TPU v7x, 512 devices: a whole 4x4x16 slice. The times are simulated.
512 devices in a mesh: dp: 16 (over y, z_lo), expert: 32 (over x, z_hi, core).
Axes of the slice: x: 4, y: 4, z: 16 (z_hi: 4, z_lo: 4; z = z_hi * 4 + z_lo), core: 2. Of those that a mesh axis runs over, the one named last changes fastest.
Arguments:
- tokens: bfloat16 [65536, 2048], P(('dp', 'expert')), may hold values from -6 to 6
- out_grad: bfloat16 [65536, 2048], P(('dp', 'expert')), may hold values from -24 to 24
- routing: int32 [65536, 2], P(('dp', 'expert')), may hold values from 0 to 31, all different within a row; in each aligned block of 128 rows (0 to 127, 128 to 255, ...) at most 9 rows name the same one
- gate_probs: float32 [65536, 2], P(('dp', 'expert')), may hold values from 0.1 to 1
- gate_up_weight: bfloat16 [32, 2048, 1536], P('expert', 'dp'), may hold values from -0.125 to 0.125
- down_weight: bfloat16 [32, 2048, 768], P('expert', 'dp'), may hold values from -0.21875 to 0.21875
Outputs:
- mixed: bfloat16 [65536, 2048], P(('dp', 'expert'))
- token_grad: bfloat16 [65536, 2048], P(('dp', 'expert'))
- down_grad: bfloat16 [32, 2048, 768], P('expert', 'dp')
Inputs may be any that keep to these rules, and one draw needn't show every extreme that they name: `routing`: the 2 ids of a row differ. Among the 128 rows of one device (aligned blocks) no id appears more than 9 times, and some id appears exactly 9 times.
All inputs are finite; a program needn't handle non-finite values.
Results may differ from a plain program's by a relative error of at most 0.018.
Values may be sent and summed in bfloat16 or wider, within the bound.
A program may use at most 64 MiB of HBM per device.

v0:
```python
import jax
import jax.numpy as jnp
from jax import lax
from jax.sharding import PartitionSpec as P

loss_scale = 0.03125


def swiglu_forward(expert_rows, gate_up_full):
    projected = jnp.dot(expert_rows, gate_up_full, preferred_element_type=jnp.float32)
    units = gate_up_full.shape[1] // 2
    gate_part = projected[:, :units]
    up_part = projected[:, units:]
    sigmoid_gate = jax.nn.sigmoid(gate_part)
    silu_gate = gate_part * sigmoid_gate
    hidden = (silu_gate * up_part).astype(jnp.bfloat16)
    return (hidden, gate_part, up_part, sigmoid_gate, silu_gate)


def weight_term(grad_rows, hidden):
    product = lax.dot_general(
        grad_rows, hidden, (((0,), (0,)), ((), ())), preferred_element_type=jnp.float32
    )
    return lax.psum_scatter(
        (product * loss_scale).astype(jnp.bfloat16), "dp", scatter_dimension=0, tiled=True
    ).astype(jnp.float32)


def shards(tokens, out_grad, routing, gate_probs, gate_up_weight, down_weight):
    peer_count = lax.axis_size("expert")
    local_count = gate_up_weight.shape[0]
    expert_count = peer_count * local_count
    tok_rows = tokens.shape[0]
    top_count = routing.shape[1]
    model_width = tokens.shape[1]
    capacity = max(2, 9 * tok_rows * top_count // (8 * expert_count))
    pair_count = tok_rows * top_count
    slot_count = expert_count * capacity
    flat_ids = routing.reshape(pair_count)
    onehot = (flat_ids[:, None] == jnp.arange(expert_count, dtype=jnp.int32)[None, :]).astype(
        jnp.int32
    )
    slot_rank = jnp.sum((jnp.cumsum(onehot, 0) - onehot) * onehot, 1)
    slot_of_pair = flat_ids * capacity + slot_rank
    pair_index = jnp.arange(pair_count, dtype=jnp.int32)
    matches = slot_of_pair[None, :] == jnp.arange(slot_count, dtype=jnp.int32)[:, None]
    filled = jnp.any(matches, axis=1)
    source = jnp.sum(jnp.where(matches, pair_index[None, :], 0), axis=1)
    token_of_slot = source // top_count
    probs_flat = gate_probs.reshape(pair_count)
    weight_slot = jnp.where(filled, probs_flat[source], jnp.float32(0.0))
    send_rows = jnp.where(filled[:, None], tokens[token_of_slot], jnp.zeros((), jnp.bfloat16))
    send_grad = (weight_slot[:, None] * out_grad[token_of_slot].astype(jnp.float32)).astype(
        jnp.bfloat16
    )
    block_shape = (peer_count, local_count * capacity, model_width)
    recv_rows, recv_grad = (
        lax.all_to_all(
            send_rows.reshape(block_shape), "expert", split_axis=0, concat_axis=0, tiled=True
        ),
        lax.all_to_all(
            send_grad.reshape(block_shape), "expert", split_axis=0, concat_axis=0, tiled=True
        ),
    )
    full_gate_up, full_down = (
        lax.all_gather(gate_up_weight, "dp", axis=1, tiled=True),
        lax.all_gather(down_weight, "dp", axis=1, tiled=True),
    )
    expert_slot = 0
    expert_rows = recv_rows.reshape(-1, model_width)
    state = swiglu_forward(expert_rows, full_gate_up[expert_slot])
    forward_state = [state]
    produced = lax.dot_general(
        state[0],
        full_down[expert_slot],
        (((1,), (1,)), ((), ())),
        preferred_element_type=jnp.float32,
    )
    output_blocks = produced.astype(jnp.bfloat16).reshape(peer_count, capacity, model_width)
    expert_slot = 0
    grad_rows = recv_grad.reshape(-1, model_width)
    hidden, gate_part, up_part, sigmoid_gate, silu_gate = forward_state[expert_slot]
    down_terms = [weight_term(grad_rows, hidden)]
    hidden_grad = jnp.dot(grad_rows, full_down[expert_slot], preferred_element_type=jnp.float32)
    pre_grad = jnp.concatenate(
        [
            hidden_grad * up_part * sigmoid_gate * (1.0 + gate_part * (1.0 - sigmoid_gate)),
            hidden_grad * silu_gate,
        ],
        axis=1,
    ).astype(jnp.bfloat16)
    input_grad = lax.dot_general(
        pre_grad,
        full_gate_up[expert_slot],
        (((1,), (1,)), ((), ())),
        preferred_element_type=jnp.float32,
    )
    grad_blocks = input_grad.astype(jnp.bfloat16).reshape(peer_count, capacity, model_width)
    returned_out, returned_grad = (
        lax.all_to_all(output_blocks, "expert", split_axis=0, concat_axis=0, tiled=True),
        lax.all_to_all(grad_blocks, "expert", split_axis=0, concat_axis=0, tiled=True),
    )
    out_pairs = returned_out.reshape(slot_count, model_width)[slot_of_pair]
    grad_pairs = returned_grad.reshape(slot_count, model_width)[slot_of_pair]
    weighted = probs_flat[:, None] * out_pairs.astype(jnp.float32)
    mixed = jnp.sum(weighted.reshape(tok_rows, top_count, model_width), axis=1).astype(jnp.bfloat16)
    token_grad = jnp.sum(
        grad_pairs.astype(jnp.float32).reshape(tok_rows, top_count, model_width), axis=1
    ).astype(jnp.bfloat16)
    down_grad = jnp.stack(down_terms, axis=0).astype(jnp.bfloat16)
    return (mixed, token_grad, down_grad)


def solution(mesh):
    in_specs = (
        P(("dp", "expert"), None),
        P(("dp", "expert"), None),
        P(("dp", "expert"), None),
        P(("dp", "expert"), None),
        P("expert", "dp", None),
        P("expert", "dp", None),
    )
    out_specs = (P(("dp", "expert"), None), P(("dp", "expert"), None), P("expert", "dp", None))
    return jax.shard_map(shards, mesh=mesh, in_specs=in_specs, out_specs=out_specs, check_vma=False)
```

profile of v0, /device:TPU:56, one launch (start us, length us, event | category | flops | bytes accessed | tf_op | source)
XLA Modules:
  0.0 740.2 jit_solution(1741571654126578607)
XLA Ops:
  7.2 0.0 copy-start
  7.2 0.0 all-gather.3.cloned.1.call-start
  7.2 0.7 all-gather.3.cloned.1.call-update
  7.9 0.8 copy.17
  8.7 0.1 eq.39
  8.8 0.1 reshape.188
  9.0 0.6 reduce-window.6
  9.6 0.2 slice_reduce_fusion
  9.8 0.8 copy.16
  10.6 0.1 reshape.193
  10.8 0.1 fusion.21
  10.9 0.2 select_reduce_fusion
  11.1 2.5 gather_fusion.2
  13.5 0.1 gather.25
  13.6 0.2 fusion.18
  13.8 0.1 broadcast_in_dim.41
  13.9 0.0 copy-done
  13.9 2.4 gather_fusion.3
  16.4 2.2 reshape.198
  18.6 3.9 multiply_convert_fusion.1
  22.5 0.0 copy-start.1
  22.5 17.3 %all-to-all-start.2 = ((bf16[32,9,2048]{2,1,0:T(8,128)(2,1)}), bf16[32,9,2048]{2,1,0:T(8,128)(2,1)}, u32[]{:S(2)}, u32[]{:S(2)}) async-start(bf16[32,9,2048]{2,1,0:T(8,128)(2,1)} %multiply_convert_fusion.1), calls=%async_computation.2 | async-start | bytes 4194304 | tf_op jit(solution)/shard_map/all_to_all | solution.py:61
  39.8 0.0 all-gather.5.cloned.1.call-start
  39.9 0.7 all-gather.5.cloned.1.call-update
  40.6 0.0 copy-done.1
  40.6 3.0 gather_fusion
  43.5 1.6 gather.22
  45.1 1.5 broadcast_select_fusion
  46.6 171.2 %all-to-all-done.2 = bf16[32,9,2048]{2,1,0:T(8,128)(2,1)} async-done(((bf16[32,9,2048]{2,1,0:T(8,128)(2,1)}), bf16[32,9,2048]{2,1,0:T(8,128)(2,1)}, u32[]{:S(2)}, u32[]{:S(2)}) %all-to-all-start.2) | async-done | bytes 1179680 | tf_op jit(solution)/shard_map/all_to_all | solution.py:61
  217.8 4.0 all-to-all-start
  221.8 2.6 reshape.194
  224.4 105.7 %all-to-all-done = bf16[32,9,2048]{2,1,0:T(8,128)(2,1)S(1)} async-done(((bf16[32,9,2048]{2,1,0:T(8,128)(2,1)}), bf16[32,9,2048]{2,1,0:T(8,128)(2,1)S(1)}, u32[]{:S(2)}, u32[]{:S(2)}) %all-to-all-start) | async-done | bytes 1179680 | tf_op jit(solution)/shard_map/all_to_all | solution.py:58
  330.2 1.3 reshape.190
  331.5 0.0 copy-start.3
  331.5 7.0 all-gather.3.cloned.1.call-done
  338.5 6.4 fusion.2
  344.8 91.6 %all-gather.5.cloned.1.call-done = bf16[1,2048,768]{2,1,0:T(8,128)(2,1)} async-done(((bf16[1,128,768]{2,1,0:T(8,128)(2,1)}), bf16[1,2048,768]{2,1,0:T(8,128)(2,1)}) %all-gather.5.cloned.1.call-update) | async-done | bytes 3145744 | tf_op jit(solution)/shard_map/all_gather | solution.py:67
  436.4 0.0 copy-done.3
  436.4 0.0 copy-start.5
  436.4 3.8 multiply_convert_fusion.3
  440.3 0.5 copy-done.5
  440.7 2.0 fusion.8
  442.7 1.6 reshape.195
  444.3 12.3 %all-to-all-start.3 = ((bf16[32,9,2048]{2,1,0:T(8,128)(2,1)}), bf16[32,9,2048]{2,1,0:T(8,128)(2,1)S(1)}, u32[]{:S(2)}, u32[]{:S(2)}) async-start(bf16[32,9,2048]{2,1,0:T(8,128)(2,1)} %reshape.195), calls=%async_computation.3 | async-start | bytes 4194304 | tf_op jit(solution)/shard_map/all_to_all | solution.py:101
  456.6 0.2 reduce-scatter.2.cloned.1.call-start
  456.9 4.8 multiply_convert_fusion
  461.6 0.0 reduce-scatter.2.cloned.1.call-update
  461.7 4.0 fusion.11
  465.7 2.7 reshape.191
  468.4 124.5 %all-to-all-done.3 = bf16[32,9,2048]{2,1,0:T(8,128)(2,1)S(1)} async-done(((bf16[32,9,2048]{2,1,0:T(8,128)(2,1)}), bf16[32,9,2048]{2,1,0:T(8,128)(2,1)S(1)}, u32[]{:S(2)}, u32[]{:S(2)}) %all-to-all-start.3) | async-done | bytes 1179680 | tf_op jit(solution)/shard_map/all_to_all | solution.py:101
  592.9 1.4 copy-done.2
  594.2 6.0 all-to-all-start.1
  600.2 0.0 copy-done.4
  600.3 0.1 copy.20
  600.4 0.1 mul.80
  600.5 1.8 reshape.196
  602.4 1.4 gather_fusion.4
  603.7 1.5 gather.28
  605.3 113.3 %all-to-all-done.1 = bf16[32,9,2048]{2,1,0:T(8,128)(2,1)} async-done(((bf16[32,9,2048]{2,1,0:T(8,128)(2,1)}), bf16[32,9,2048]{2,1,0:T(8,128)(2,1)}, u32[]{:S(2)}, u32[]{:S(2)}) %all-to-all-start.1) | async-done | bytes 1179680 | tf_op jit(solution)/shard_map/all_to_all | solution.py:100
  718.6 1.8 reshape.192
  720.4 2.3 gather_fusion.1
  722.8 2.4 reshape.197
  725.1 4.6 reduce_sum.48
  729.7 3.9 multiply_reduce_fusion
  (13 shorter events, 0.1 us)
Async XLA Ops:
  7.2 6.7 copy-start
  7.2 331.3 %all-gather.3.cloned.1.call-start = ((), (), s32[]{:S(2)}) async-start(), calls=%async_computation.5 | async-start | bytes 6684672 | tf_op jit(solution)/shard_map/all_gather | solution.py:66
  22.5 18.1 %copy-start.1 = (bf16[128,2048]{1,0:T(8,128)(2,1)S(1)}, bf16[128,2048]{1,0:T(8,128)(2,1)}, u32[]{:S(2)}) copy-start(bf16[128,2048]{1,0:T(8,128)(2,1)} %param.6) | copy-start | bytes 1572868
  22.5 195.3 %all-to-all-start.2 = ((bf16[32,9,2048]{2,1,0:T(8,128)(2,1)}), bf16[32,9,2048]{2,1,0:T(8,128)(2,1)}, u32[]{:S(2)}, u32[]{:S(2)}) async-start(bf16[32,9,2048]{2,1,0:T(8,128)(2,1)} %multiply_convert_fusion.1), calls=%async_computation.2 | async-start | bytes 4194304 | tf_op jit(solution)/shard_map/all_to_all | solution.py:61
  39.8 396.6 %all-gather.5.cloned.1.call-start = ((), (), s32[]{:S(2)}) async-start(), calls=%async_computation.6 | async-start | bytes 3342336 | tf_op jit(solution)/shard_map/all_gather | solution.py:67
  217.8 112.4 %all-to-all-start = ((bf16[32,9,2048]{2,1,0:T(8,128)(2,1)}), bf16[32,9,2048]{2,1,0:T(8,128)(2,1)S(1)}, u32[]{:S(2)}, u32[]{:S(2)}) async-start(bf16[32,9,2048]{2,1,0:T(8,128)(2,1)} %broadcast_select_fusion), calls=%async_computation | async-start | bytes 4194304 | tf_op jit(solution)/shard_map/all_to_all | solution.py:58
  331.5 104.9 %copy-start.3 = (bf16[288,2048]{1,0:T(8,128)(2,1)S(1)}, bf16[288,2048]{1,0:T(8,128)(2,1)}, u32[]{:S(2)}) copy-start(bf16[288,2048]{1,0:T(8,128)(2,1)} %reshape.194) | copy-start | bytes 3538948
  436.4 4.3 copy-start.5
  444.3 148.6 %all-to-all-start.3 = ((bf16[32,9,2048]{2,1,0:T(8,128)(2,1)}), bf16[32,9,2048]{2,1,0:T(8,128)(2,1)S(1)}, u32[]{:S(2)}, u32[]{:S(2)}) async-start(bf16[32,9,2048]{2,1,0:T(8,128)(2,1)} %reshape.195), calls=%async_computation.3 | async-start | bytes 4194304 | tf_op jit(solution)/shard_map/all_to_all | solution.py:101
  456.6 277.0 %reduce-scatter.2.cloned.1.call-start = ((), (), s32[]{:S(2)}) async-start(), calls=%async_computation.7 | async-start | bytes 3342336 | tf_op jit(solution)/shard_map/reduce_scatter | solution.py:24
  468.4 131.9 %copy-start.4 = (s32[128,2]{0,1:T(2,128)S(1)}, s32[128,2]{0,1:T(2,128)}, u32[]{:S(2)}) copy-start(s32[128,2]{0,1:T(2,128)} %param.8) | copy-start | bytes 3076
  592.9 1.4 copy-start.2
  594.2 124.4 %all-to-all-start.1 = ((bf16[32,9,2048]{2,1,0:T(8,128)(2,1)}), bf16[32,9,2048]{2,1,0:T(8,128)(2,1)}, u32[]{:S(2)}, u32[]{:S(2)}) async-start(bf16[32,9,2048]{2,1,0:T(8,128)(2,1)} %reshape.191), calls=%async_computation.1 | async-start | bytes 4194304 | tf_op jit(solution)/shard_map/all_to_all | solution.py:100
Sparse Core Ops, SparseCore 0:
  10.1 328.3 all-gather.2
  340.6 95.8 all-gather.4
  461.8 251.0 reduce-scatter.1
where the time goes:
time: 741 us; the launch traced here: 740 us
  waiting for transfers between devices  615 us (83%)
  starting transfers between devices  39.9 us (5%)
  local copies, waits for them, and re-layouts  35.6 us (5%)
  matrix products  21 us (3%)
  other arithmetic  15 us (2%)
  between operations  14 us (2%)
    all_to_all x1, waiting for transfers between devices, shards(): lax.all_to_all(send_grad.reshape(block_shape), 'expert', split_axis=0, co...  171 us
    all_to_all x1, waiting for transfers between devices, shards(): lax.all_to_all(grad_blocks, 'expert', split_axis=0, concat_axis=0, tiled=...  124 us
    all_to_all x1, waiting for transfers between devices, shards(): lax.all_to_all(output_blocks, 'expert', split_axis=0, concat_axis=0, tile...  113 us
    all_to_all x1, waiting for transfers between devices, shards(): lax.all_to_all(send_rows.reshape(block_shape), 'expert', split_axis=0, co...  106 us
    all_gather x1, waiting for transfers between devices, shards(): lax.all_gather(down_weight, 'dp', axis=1, tiled=True)  91.6 us
    all_to_all x1, starting transfers between devices, shards(): lax.all_to_all(send_grad.reshape(block_shape), 'expert', split_axis=0, co...  17.3 us
  transfers between devices with their start and end apart: 7, of which 6 were waited for; matrix products, arithmetic and copies ran while one was open for 8% of the time, Pallas kernels for 0%

commit v1 on v0

--- a/solution.py
+++ b/solution.py
@@ -21,9 +21,18 @@
     product = lax.dot_general(
         grad_rows, hidden, (((0,), (0,)), ((), ())), preferred_element_type=jnp.float32
     )
-    return lax.psum_scatter(
-        (product * loss_scale).astype(jnp.bfloat16), "dp", scatter_dimension=0, tiled=True
-    ).astype(jnp.float32)
+    parts = lax.axis_size("dp")
+    blocks = (product * loss_scale).astype(jnp.bfloat16)
+    blocks = blocks.reshape(parts, blocks.shape[0] // parts, blocks.shape[1])
+    received = lax.all_to_all(blocks, "dp", split_axis=0, concat_axis=0, tiled=True)
+    return jnp.sum(received.astype(jnp.float32), axis=0)
+
+
+def gather_rows(local):
+    parts = lax.axis_size("dp")
+    copies = jnp.broadcast_to(local[None], (parts,) + local.shape)
+    received = lax.all_to_all(copies, "dp", split_axis=0, concat_axis=0, tiled=True)
+    return received.reshape(parts * local.shape[0], local.shape[1])
 
 
 def shards(tokens, out_grad, routing, gate_probs, gate_up_weight, down_weight):
@@ -62,10 +71,11 @@
             send_grad.reshape(block_shape), "expert", split_axis=0, concat_axis=0, tiled=True
         ),
     )
-    full_gate_up, full_down = (
-        lax.all_gather(gate_up_weight, "dp", axis=1, tiled=True),
-        lax.all_gather(down_weight, "dp", axis=1, tiled=True),
-    )
+    gate_width = gate_up_weight.shape[2]
+    joined = jnp.concatenate([gate_up_weight[0], down_weight[0]], axis=1)
+    full_joined = gather_rows(joined)
+    full_gate_up = full_joined[None, :, :gate_width]
+    full_down = full_joined[None, :, gate_width:]
     expert_slot = 0
     expert_rows = recv_rows.reshape(-1, model_width)
     state = swiglu_forward(expert_rows, full_gate_up[expert_slot])

time: 741 us -> 760 us (1.026)
  the two profiles are of different devices: /device:TPU:56 before, /device:TPU:2 now
where the time goes in v1:
time: 760 us; the launch traced here: 759 us
  waiting for transfers between devices  616 us (81%)
  starting transfers between devices  60.7 us (8%)
  local copies, waits for them, and re-layouts  41 us (5%)
  matrix products  22.5 us (3%)
  other arithmetic  18.1 us (2%)
    all_to_all x1, waiting for transfers between devices, gather_rows(): lax.all_to_all(copies, 'dp', split_axis=0, concat_axis=0, tiled=True)  205 us
    all_to_all x1, waiting for transfers between devices, shards(): lax.all_to_all(send_grad.reshape(block_shape), 'expert', split_axis=0, co...  94.7 us
    all_to_all x1, waiting for transfers between devices, shards(): lax.all_to_all(grad_blocks, 'expert', split_axis=0, concat_axis=0, tiled=...  92.1 us
    all_to_all x1, waiting for transfers between devices, shards(): lax.all_to_all(output_blocks, 'expert', split_axis=0, concat_axis=0, tile...  88 us
    all_to_all x1, waiting for transfers between devices, shards(): lax.all_to_all(send_rows.reshape(block_shape), 'expert', split_axis=0, co...  81.6 us
    all_to_all x1, waiting for transfers between devices, weight_term(): lax.all_to_all(blocks, 'dp', split_axis=0, concat_axis=0, tiled=True)  54.9 us
    all_to_all x1, starting transfers between devices, shards(): lax.all_to_all(send_rows.reshape(block_shape), 'expert', split_axis=0, co...  18.4 us
  transfers between devices with their start and end apart: 6, of which 6 were waited for; matrix products, arithmetic and copies ran while one was open for 7% of the time, Pallas kernels for 0%

profile of v1, /device:TPU:2, one launch (start us, length us, event | category | flops | bytes accessed | tf_op | source)
XLA Modules:
  0.0 759.2 jit_solution(7917935842740808387)
XLA Ops:
  0.6 0.0 copy-start
  0.6 0.8 copy.17
  1.5 0.1 reshape.203
  1.6 0.1 eq.39
  1.8 0.6 reduce-window.6
  2.4 0.2 slice_reduce_fusion
  2.6 0.1 fusion.21
  2.7 0.2 select_reduce_fusion
  2.9 0.2 fusion.18
  3.1 0.0 copy-done
  3.1 3.0 gather_fusion
  6.0 1.6 gather.22
  7.6 0.1 broadcast_in_dim.32
  7.7 1.5 broadcast_select_fusion
  9.3 18.4 %all-to-all-start = ((bf16[32,9,2048]{2,1,0:T(8,128)(2,1)}), bf16[32,9,2048]{2,1,0:T(8,128)(2,1)S(1)}, u32[]{:S(2)}, u32[]{:S(2)}) async-start(bf16[32,9,2048]{2,1,0:T(8,128)(2,1)} %broadcast_select_fusion), calls=%async_computation | async-start | bytes 4194304 | tf_op jit(solution)/shard_map/all_to_all | solution.py:67
  27.7 0.0 copy-done.2
  27.7 3.0 gather_fusion.3
  30.6 3.2 reshape.215
  33.8 0.0 copy-done.10
  33.8 0.1 copy.16
  33.9 0.1 reshape.209
  34.1 2.5 gather_fusion.2
  36.5 0.1 gather.25
  36.7 3.8 multiply_convert_fusion.1
  40.5 81.6 %all-to-all-done = bf16[32,9,2048]{2,1,0:T(8,128)(2,1)S(1)} async-done(((bf16[32,9,2048]{2,1,0:T(8,128)(2,1)}), bf16[32,9,2048]{2,1,0:T(8,128)(2,1)S(1)}, u32[]{:S(2)}, u32[]{:S(2)}) %all-to-all-start) | async-done | bytes 1179680 | tf_op jit(solution)/shard_map/all_to_all | solution.py:67
  122.1 11.4 %all-to-all-start.3 = ((bf16[32,9,2048]{2,1,0:T(8,128)(2,1)}), bf16[32,9,2048]{2,1,0:T(8,128)(2,1)}, u32[]{:S(2)}, u32[]{:S(2)}) async-start(bf16[32,9,2048]{2,1,0:T(8,128)(2,1)} %multiply_convert_fusion.1), calls=%async_computation.3 | async-start | bytes 4194304 | tf_op jit(solution)/shard_map/all_to_all | solution.py:70
  133.6 0.0 copy-done.7
  133.6 0.0 copy-done.8
  133.6 94.7 %all-to-all-done.3 = bf16[32,9,2048]{2,1,0:T(8,128)(2,1)} async-done(((bf16[32,9,2048]{2,1,0:T(8,128)(2,1)}), bf16[32,9,2048]{2,1,0:T(8,128)(2,1)}, u32[]{:S(2)}, u32[]{:S(2)}) %all-to-all-start.3) | async-done | bytes 1179680 | tf_op jit(solution)/shard_map/all_to_all | solution.py:70
  228.3 4.6 broadcast_in_dim.52
  232.9 11.2 %all-to-all-start.1 = ((bf16[16,128,2304]{2,1,0:T(8,128)(2,1)}), bf16[16,128,2304]{2,1,0:T(8,128)(2,1)}, u32[]{:S(2)}, u32[]{:S(2)}) async-start(bf16[16,128,2304]{2,1,0:T(8,128)(2,1)} %broadcast_in_dim.52), calls=%async_computation.1 | async-start | bytes 18874368 | tf_op jit(solution)/shard_map/all_to_all | solution.py:34
  244.1 1.4 reshape.205
  245.4 1.9 reshape.210
  247.4 0.0 copy-start.5
  247.4 204.7 %all-to-all-done.1 = bf16[16,128,2304]{2,1,0:T(8,128)(2,1)} async-done(((bf16[16,128,2304]{2,1,0:T(8,128)(2,1)}), bf16[16,128,2304]{2,1,0:T(8,128)(2,1)}, u32[]{:S(2)}, u32[]{:S(2)}) %all-to-all-start.1) | async-done | bytes 9437216 | tf_op jit(solution)/shard_map/all_to_all | solution.py:34
  452.1 0.0 copy-done.6
  452.1 4.8 fusion.2
  456.8 0.0 copy-done.5
  456.9 4.0 multiply_convert_fusion.3
  460.8 3.0 fusion.11
  463.8 1.6 reshape.207
  465.4 6.7 all-to-all-start.2
  472.1 6.0 fusion.8
  478.2 2.7 reshape.211
  480.8 88.0 %all-to-all-done.2 = bf16[32,9,2048]{2,1,0:T(8,128)(2,1)S(1)} async-done(((bf16[32,9,2048]{2,1,0:T(8,128)(2,1)}), bf16[32,9,2048]{2,1,0:T(8,128)(2,1)S(1)}, u32[]{:S(2)}, u32[]{:S(2)}) %all-to-all-start.2) | async-done | bytes 1179680 | tf_op jit(solution)/shard_map/all_to_all | solution.py:110
  568.9 1.4 copy-done.3
  570.3 8.3 %all-to-all-start.4 = ((bf16[32,9,2048]{2,1,0:T(8,128)(2,1)}), bf16[32,9,2048]{2,1,0:T(8,128)(2,1)}, u32[]{:S(2)}, u32[]{:S(2)}) async-start(bf16[32,9,2048]{2,1,0:T(8,128)(2,1)} %reshape.211), calls=%async_computation.4 | async-start | bytes 4194304 | tf_op jit(solution)/shard_map/all_to_all | solution.py:111
  578.6 4.8 multiply_convert_fusion
  583.4 92.1 %all-to-all-done.4 = bf16[32,9,2048]{2,1,0:T(8,128)(2,1)} async-done(((bf16[32,9,2048]{2,1,0:T(8,128)(2,1)}), bf16[32,9,2048]{2,1,0:T(8,128)(2,1)}, u32[]{:S(2)}, u32[]{:S(2)}) %all-to-all-start.4) | async-done | bytes 1179680 | tf_op jit(solution)/shard_map/all_to_all | solution.py:111
  675.5 4.6 all-to-all-start.5
  680.1 0.0 copy-done.9
  680.1 0.1 copy.20
  680.2 0.1 mul.80
  680.4 1.8 reshape.208
  682.2 1.4 gather_fusion.1
  683.6 2.3 reshape.214
  685.9 1.8 reshape.212
  687.7 2.4 gather_fusion.4
  690.1 2.7 gather.28
  692.8 4.6 reduce_sum.60
  697.3 0.0 copy-done.4
  697.3 3.9 multiply_reduce_fusion
  701.3 54.9 %all-to-all-done.5 = bf16[16,128,768]{2,1,0:T(8,128)(2,1)} async-done(((bf16[16,128,768]{2,1,0:T(8,128)(2,1)}), bf16[16,128,768]{2,1,0:T(8,128)(2,1)}, u32[]{:S(2)}, u32[]{:S(2)}) %all-to-all-start.5) | async-done | bytes 3145760 | tf_op jit(solution)/shard_map/all_to_all | solution.py:27
  756.1 3.1 reduce_sum.61
  (21 shorter events, 0.2 us)
Async XLA Ops:
  0.6 2.4 copy-start
  9.3 18.4 %copy-start.2 = (bf16[128,2048]{1,0:T(8,128)(2,1)S(1)}, bf16[128,2048]{1,0:T(8,128)(2,1)}, u32[]{:S(2)}) copy-start(bf16[128,2048]{1,0:T(8,128)(2,1)} %param.7) | copy-start | bytes 1572868
  9.3 112.8 %all-to-all-start = ((bf16[32,9,2048]{2,1,0:T(8,128)(2,1)}), bf16[32,9,2048]{2,1,0:T(8,128)(2,1)S(1)}, u32[]{:S(2)}, u32[]{:S(2)}) async-start(bf16[32,9,2048]{2,1,0:T(8,128)(2,1)} %broadcast_select_fusion), calls=%async_computation | async-start | bytes 4194304 | tf_op jit(solution)/shard_map/all_to_all | solution.py:67
  30.6 3.2 copy-start.10
  40.5 93.1 %copy-start.7 = (bf16[1,128,1536]{2,1,0:T(8,128)(2,1)S(1)}, bf16[1,128,1536]{2,1,0:T(8,128)(2,1)}, u32[]{:S(2)}) copy-start(bf16[1,128,1536]{2,1,0:T(8,128)(2,1)} %param.10) | copy-start | bytes 1179652
  40.5 93.1 %copy-start.8 = (bf16[1,128,768]{2,1,0:T(8,128)(2,1)S(1)}, bf16[1,128,768]{2,1,0:T(8,128)(2,1)}, u32[]{:S(2)}) copy-start(bf16[1,128,768]{2,1,0:T(8,128)(2,1)} %param.11) | copy-start | bytes 589828
  122.1 106.2 %all-to-all-start.3 = ((bf16[32,9,2048]{2,1,0:T(8,128)(2,1)}), bf16[32,9,2048]{2,1,0:T(8,128)(2,1)}, u32[]{:S(2)}, u32[]{:S(2)}) async-start(bf16[32,9,2048]{2,1,0:T(8,128)(2,1)} %multiply_convert_fusion.1), calls=%async_computation.3 | async-start | bytes 4194304 | tf_op jit(solution)/shard_map/all_to_all | solution.py:70
  232.9 219.2 %all-to-all-start.1 = ((bf16[16,128,2304]{2,1,0:T(8,128)(2,1)}), bf16[16,128,2304]{2,1,0:T(8,128)(2,1)}, u32[]{:S(2)}, u32[]{:S(2)}) async-start(bf16[16,128,2304]{2,1,0:T(8,128)(2,1)} %broadcast_in_dim.52), calls=%async_computation.1 | async-start | bytes 18874368 | tf_op jit(solution)/shard_map/all_to_all | solution.py:34
  245.4 206.6 %copy-start.6 = (bf16[288,2048]{1,0:T(8,128)(2,1)S(1)}, bf16[288,2048]{1,0:T(8,128)(2,1)}, u32[]{:S(2)}) copy-start(bf16[288,2048]{1,0:T(8,128)(2,1)} %reshape.205) | copy-start | bytes 3538948
  247.4 209.5 %copy-start.5 = (bf16[288,2048]{1,0:T(8,128)(2,1)}, bf16[288,2048]{1,0:T(8,128)(2,1)S(1)}, u32[]{:S(2)}) copy-start(bf16[288,2048]{1,0:T(8,128)(2,1)S(1)} %reshape.210) | copy-start | bytes 3538948
  465.4 103.5 %all-to-all-start.2 = ((bf16[32,9,2048]{2,1,0:T(8,128)(2,1)}), bf16[32,9,2048]{2,1,0:T(8,128)(2,1)S(1)}, u32[]{:S(2)}, u32[]{:S(2)}) async-start(bf16[32,9,2048]{2,1,0:T(8,128)(2,1)} %reshape.207), calls=%async_computation.2 | async-start | bytes 4194304 | tf_op jit(solution)/shard_map/all_to_all | solution.py:110
  568.9 1.4 copy-start.3
  570.3 105.2 %all-to-all-start.4 = ((bf16[32,9,2048]{2,1,0:T(8,128)(2,1)}), bf16[32,9,2048]{2,1,0:T(8,128)(2,1)}, u32[]{:S(2)}, u32[]{:S(2)}) async-start(bf16[32,9,2048]{2,1,0:T(8,128)(2,1)} %reshape.211), calls=%async_computation.4 | async-start | bytes 4194304 | tf_op jit(solution)/shard_map/all_to_all | solution.py:111
  675.5 4.6 copy-start.9
  675.5 80.7 %all-to-all-start.5 = ((bf16[16,128,768]{2,1,0:T(8,128)(2,1)}), bf16[16,128,768]{2,1,0:T(8,128)(2,1)}, u32[]{:S(2)}, u32[]{:S(2)}) async-start(bf16[16,128,768]{2,1,0:T(8,128)(2,1)} %bitcast.31), calls=%async_computation.5 | async-start | bytes 6291456 | tf_op jit(solution)/shard_map/all_to_all | solution.py:27
  690.1 7.3 copy-start.4
  697.3 61.9 %copy-start.1 = (bf16[128,2048]{1,0:T(8,128)(2,1)S(1)}, bf16[128,2048]{1,0:T(8,128)(2,1)}, u32[]{:S(2)}) copy-start(bf16[128,2048]{1,0:T(8,128)(2,1)} %param.6) | copy-start | bytes 1572868

commit v2 on v1

v2 whole, which is shorter than its diff:
```python
import functools

import jax
import jax.numpy as jnp
from jax import lax
from jax.experimental import pallas as pl
from jax.experimental.pallas import tpu as pltpu
from jax.sharding import PartitionSpec as P

MESH = pl.DeviceIdType.MESH

loss_scale = 0.03125


def exchange_kernel(n_dp, n_ex, bcast, ex_send, dp_send, ex_recv, dp_recv, send_sems, recv_sems, own_sems):
    q = lax.axis_index("dp")
    p = lax.axis_index("expert")
    barrier = pltpu.get_barrier_semaphore()

    def greet_ex(k, c):
        pl.semaphore_signal(barrier, 1, device_id=(q, lax.rem(p + k, n_ex)), device_id_type=MESH)
        return c

    def greet_dp(k, c):
        pl.semaphore_signal(barrier, 1, device_id=(lax.rem(q + k, n_dp), p), device_id_type=MESH)
        return c

    lax.fori_loop(1, n_ex, greet_ex, 0)
    lax.fori_loop(1, n_dp, greet_dp, 0)
    pl.semaphore_wait(barrier, n_ex + n_dp - 2)

    def ex_copy(j, slot):
        return pltpu.make_async_remote_copy(
            src_ref=ex_send.at[j], dst_ref=ex_recv.at[slot], send_sem=send_sems.at[j],
            recv_sem=recv_sems.at[slot], device_id=(q, j), device_id_type=MESH)

    def dp_copy(i, slot):
        src = dp_send if bcast else dp_send.at[i]
        return pltpu.make_async_remote_copy(
            src_ref=src, dst_ref=dp_recv.at[slot], send_sem=send_sems.at[n_ex + i],
            recv_sem=recv_sems.at[n_ex + slot], device_id=(i, p), device_id_type=MESH)

    def send_ex(k, c):
        ex_copy(lax.rem(p + k, n_ex), p).start()
        return c

    def send_dp(k, c):
        dp_copy(lax.rem(q + k, n_dp), q).start()
        return c

    lax.fori_loop(1, n_dp, send_dp, 0)
    lax.fori_loop(1, n_ex, send_ex, 0)
    own_ex = pltpu.make_async_copy(ex_send.at[p], ex_recv.at[p], own_sems.at[0])
    own_dp = pltpu.make_async_copy(dp_send if bcast else dp_send.at[q], dp_recv.at[q], own_sems.at[1])
    own_ex.start()
    own_dp.start()

    def wait_ex(k, c):
        j = lax.rem(p + k, n_ex)
        ex_copy(j, p).wait_send()
        ex_copy(j, j).wait_recv()
        return c

    def wait_dp(k, c):
        i = lax.rem(q + k, n_dp)
        dp_copy(i, q).wait_send()
        dp_copy(i, i).wait_recv()
        return c

    lax.fori_loop(1, n_ex, wait_ex, 0)
    lax.fori_loop(1, n_dp, wait_dp, 0)
    own_ex.wait()
    own_dp.wait()


def exchange(ex_send, dp_send, bcast, cid):
    n_dp = lax.axis_size("dp")
    n_ex = lax.axis_size("expert")
    dp_block = dp_send.shape if bcast else dp_send.shape[1:]
    return pl.pallas_call(
        functools.partial(exchange_kernel, n_dp, n_ex, bcast),
        out_shape=(
            jax.ShapeDtypeStruct(ex_send.shape, ex_send.dtype),
            jax.ShapeDtypeStruct((n_dp,) + tuple(dp_block), dp_send.dtype),
        ),
        in_specs=[pl.BlockSpec(memory_space=pl.ANY)] * 2,
        out_specs=(pl.BlockSpec(memory_space=pl.ANY), pl.BlockSpec(memory_space=pl.ANY)),
        scratch_shapes=[
            pltpu.SemaphoreType.DMA((n_ex + n_dp,)),
            pltpu.SemaphoreType.DMA((n_ex + n_dp,)),
            pltpu.SemaphoreType.DMA((2,)),
        ],
        compiler_params=pltpu.CompilerParams(collective_id=cid, has_side_effects=True),
    )(ex_send, dp_send)


def swiglu_forward(expert_rows, gate_up_full):
    projected = jnp.dot(expert_rows, gate_up_full, preferred_element_type=jnp.float32)
    units = gate_up_full.shape[1] // 2
    gate_part = projected[:, :units]
    up_part = projected[:, units:]
    sigmoid_gate = jax.nn.sigmoid(gate_part)
    silu_gate = gate_part * sigmoid_gate
    hidden = (silu_gate * up_part).astype(jnp.bfloat16)
    return (hidden, gate_part, up_part, sigmoid_gate, silu_gate)


def weight_blocks(grad_rows, hidden):
    product = lax.dot_general(
        grad_rows, hidden, (((0,), (0,)), ((), ())), preferred_element_type=jnp.float32
    )
    parts = lax.axis_size("dp")
    blocks = (product * loss_scale).astype(jnp.bfloat16)
    return blocks.reshape(parts, blocks.shape[0] // parts, blocks.shape[1])


def shards(tokens, out_grad, routing, gate_probs, gate_up_weight, down_weight):
    peer_count = lax.axis_size("expert")
    local_count = gate_up_weight.shape[0]
    expert_count = peer_count * local_count
    tok_rows = tokens.shape[0]
    top_count = routing.shape[1]
    model_width = tokens.shape[1]
    capacity = max(2, 9 * tok_rows * top_count // (8 * expert_count))
    pair_count = tok_rows * top_count
    slot_count = expert_count * capacity
    flat_ids = routing.reshape(pair_count)
    onehot = (flat_ids[:, None] == jnp.arange(expert_count, dtype=jnp.int32)[None, :]).astype(
        jnp.int32
    )
    slot_rank = jnp.sum((jnp.cumsum(onehot, 0) - onehot) * onehot, 1)
    slot_of_pair = flat_ids * capacity + slot_rank
    pair_index = jnp.arange(pair_count, dtype=jnp.int32)
    matches = slot_of_pair[None, :] == jnp.arange(slot_count, dtype=jnp.int32)[:, None]
    filled = jnp.any(matches, axis=1)
    source = jnp.sum(jnp.where(matches, pair_index[None, :], 0), axis=1)
    token_of_slot = source // top_count
    probs_flat = gate_probs.reshape(pair_count)
    weight_slot = jnp.where(filled, probs_flat[source], jnp.float32(0.0))
    send_rows = jnp.where(filled[:, None], tokens[token_of_slot], jnp.zeros((), jnp.bfloat16))
    send_grad = (weight_slot[:, None] * out_grad[token_of_slot].astype(jnp.float32)).astype(
        jnp.bfloat16
    )
    block_shape = (peer_count, local_count * capacity, 2 * model_width)
    send_both = jnp.concatenate([send_rows, send_grad], axis=1).reshape(block_shape)
    gate_width = gate_up_weight.shape[2]
    joined = jnp.concatenate([gate_up_weight[0], down_weight[0]], axis=1)
    recv_both, gathered = exchange(send_both, joined, True, 0)
    recv_both = recv_both.reshape(-1, 2 * model_width)
    expert_rows = recv_both[:, :model_width]
    grad_rows = recv_both[:, model_width:]
    full_joined = gathered.reshape(-1, joined.shape[1])
    full_gate_up = full_joined[:, :gate_width]
    full_down = full_joined[:, gate_width:]
    hidden, gate_part, up_part, sigmoid_gate, silu_gate = swiglu_forward(expert_rows, full_gate_up)
    produced = lax.dot_general(
        hidden, full_down, (((1,), (1,)), ((), ())), preferred_element_type=jnp.float32
    )
    down_parts = weight_blocks(grad_rows, hidden)
    hidden_grad = jnp.dot(grad_rows, full_down, preferred_element_type=jnp.float32)
    pre_grad = jnp.concatenate(
        [
            hidden_grad * up_part * sigmoid_gate * (1.0 + gate_part * (1.0 - sigmoid_gate)),
            hidden_grad * silu_gate,
        ],
        axis=1,
    ).astype(jnp.bfloat16)
    input_grad = lax.dot_general(
        pre_grad, full_gate_up, (((1,), (1,)), ((), ())), preferred_element_type=jnp.float32
    )
    back_both = jnp.concatenate(
        [produced.astype(jnp.bfloat16), input_grad.astype(jnp.bfloat16)], axis=1
    ).reshape(block_shape)
    returned, down_recv = exchange(back_both, down_parts, False, 1)
    returned = returned.reshape(slot_count, 2 * model_width)
    out_pairs = returned[:, :model_width][slot_of_pair]
    grad_pairs = returned[:, model_width:][slot_of_pair]
    weighted = probs_flat[:, None] * out_pairs.astype(jnp.float32)
    mixed = jnp.sum(weighted.reshape(tok_rows, top_count, model_width), axis=1).astype(jnp.bfloat16)
    token_grad = jnp.sum(
        grad_pairs.astype(jnp.float32).reshape(tok_rows, top_count, model_width), axis=1
    ).astype(jnp.bfloat16)
    down_grad = jnp.sum(down_recv.astype(jnp.float32), axis=0)[None].astype(jnp.bfloat16)
    return (mixed, token_grad, down_grad)


def solution(mesh):
    in_specs = (
        P(("dp", "expert"), None),
        P(("dp", "expert"), None),
        P(("dp", "expert"), None),
        P(("dp", "expert"), None),
        P("expert", "dp", None),
        P("expert", "dp", None),
    )
    out_specs = (P(("dp", "expert"), None), P(("dp", "expert"), None), P("expert", "dp", None))
    return jax.shard_map(shards, mesh=mesh, in_specs=in_specs, out_specs=out_specs, check_vma=False)
```

time: 760 us -> 743 us (0.978)
  the two profiles are of different devices: /device:TPU:2 before, /device:TPU:39 now
where the time goes in v2:
time: 743 us
  Pallas kernels  671 us (90%)
  local copies, waits for them, and re-layouts  36.9 us (5%)
  other arithmetic  21.3 us (3%)
  matrix products  13 us (2%)
    pallas_call x2, Pallas kernels, exchange(): pl.pallas_call(functools.partial(exchange_kernel, n_dp, n_ex, bcast), out...  671 us

profile of v2, /device:TPU:39, one launch (start us, length us, event | category | flops | bytes accessed | tf_op | source)
XLA Modules:
  0.0 742.7 jit_solution(10228586398833121262)
XLA Ops:
  0.6 0.0 copy-start
  0.6 0.8 copy.17
  1.5 0.1 eq.39
  1.6 0.6 reduce-window.6
  2.2 0.2 slice_reduce_fusion
  2.5 0.1 reshape.194
  2.6 0.1 fusion.24
  2.7 0.2 select_reduce_fusion
  2.9 0.8 copy.16
  3.7 0.1 reshape.196
  3.9 2.5 gather_fusion.1
  6.3 0.1 gather.24
  6.4 0.2 fusion.21
  6.6 0.1 broadcast_in_dim.42
  6.7 0.0 copy-done
  6.7 2.4 gather_fusion.2
  9.2 2.1 reshape.202
  11.3 0.0 copy-start.2
  11.3 3.9 multiply_convert_fusion.1
  15.2 0.0 copy-done.2
  15.2 3.0 gather_fusion
  18.1 1.6 gather.22
  19.7 0.0 copy-start.3
  19.7 0.2 broadcast_select_fusion
  19.9 1.4 copy-done.3
  21.3 0.0 copy-start.4
  21.3 0.0 copy-start.5
  21.3 2.9 pad_maximum_fusion.ex_send
  24.1 0.0 copy-done.4
  24.1 0.0 copy-done.5
  24.1 0.9 pad_maximum_fusion.2.dp_send
  25.0 400.4 %shard_map.85 = (bf16[32,9,4096]{2,1,0:T(8,128)(2,1)}, bf16[16,128,2304]{2,1,0:T(8,128)(2,1)}) custom-call(bf16[32,9,4096]{2,1,0:T(8,128)(2,1)} %pad_maximum_fusion.ex_send, bf16[128,2304]{1,0:T(8,128)(2,1)} %pad_maximum_fusion.2.dp_send), custom_call_target="tpu_custom_call" | custom-call | tf_op jit(solution)/shard_map/pallas_call | solution.py:80
  425.4 3.4 reshape.197
  428.8 0.0 copy-start.7
  428.8 4.9 fusion.2
  433.7 0.6 copy-done.7
  434.3 1.4 multiply_convert_fusion.3
  435.7 3.6 multiply_convert_fusion
  439.2 1.1 fusion.11
  440.4 2.0 fusion.8
  442.4 0.2 pad_maximum_fusion.1
  442.6 2.8 reshape.199.ex_send
  445.4 270.2 %shard_map.86 = (bf16[32,9,4096]{2,1,0:T(8,128)(2,1)}, bf16[16,128,768]{2,1,0:T(8,128)(2,1)}) custom-call(bf16[32,9,4096]{2,1,0:T(8,128)(2,1)} %reshape.199.ex_send, bf16[16,128,768]{2,1,0:T(8,128)(2,1)} %bitcast.28), custom_call_target="tpu_custom_call" | custom-call | tf_op jit(solution)/shard_map/pallas_call | solution.py:80
  715.6 4.9 reshape.201
  720.4 0.0 copy-start.6
  720.4 1.8 fusion.29
  722.2 0.0 copy-done.6
  722.3 0.1 copy.21
  722.4 0.1 mul.89
  722.5 2.3 gather_fusion.3
  724.9 3.4 reshape.203
  728.3 5.6 multiply_reduce_fusion
  733.9 1.4 gather_fusion.4
  735.2 0.0 copy-start.1
  735.2 0.7 gather.28
  736.0 3.6 reduce_sum.60
  739.6 3.0 reduce_sum.61
  742.6 0.0 copy-done.1
  (10 shorter events, 0.1 us)
Async XLA Ops:
  0.6 6.1 copy-start
  11.3 3.9 copy-start.2
  19.7 1.6 copy-start.3
  21.3 2.9 copy-start.4
  21.3 2.9 copy-start.5
  428.8 5.5 copy-start.7
  720.4 1.8 copy-start.6
  735.2 7.4 copy-start.1

commit v3 on v2

--- a/solution.py
+++ b/solution.py
@@ -12,9 +12,12 @@
 loss_scale = 0.03125
 
 
-def exchange_kernel(n_dp, n_ex, bcast, ex_send, dp_send, ex_recv, dp_recv, send_sems, recv_sems, own_sems):
+def exchange_kernel(n_dp, n_ex, n_lo, bcast, ex_send, dp_send, ex_recv, dp_recv, send_sems, recv_sems, own_sems):
     q = lax.axis_index("dp")
     p = lax.axis_index("expert")
+    n_hi = n_dp // n_lo
+    row = q // n_lo
+    lo = q % n_lo
     barrier = pltpu.get_barrier_semaphore()
 
     def greet_ex(k, c):
@@ -40,6 +43,13 @@
             src_ref=src, dst_ref=dp_recv.at[slot], send_sem=send_sems.at[n_ex + i],
             recv_sem=recv_sems.at[n_ex + slot], device_id=(i, p), device_id_type=MESH)
 
+    def row_copy(r, slot_row, k):
+        rows = pl.ds(pl.multiple_of(slot_row * n_lo, n_lo), n_lo)
+        return pltpu.make_async_remote_copy(
+            src_ref=dp_recv.at[rows], dst_ref=dp_recv.at[rows],
+            send_sem=send_sems.at[n_ex + n_dp + k], recv_sem=recv_sems.at[n_ex + n_dp + slot_row],
+            device_id=(r * n_lo + lo, p), device_id_type=MESH)
+
     def send_ex(k, c):
         ex_copy(lax.rem(p + k, n_ex), p).start()
         return c
@@ -48,12 +58,19 @@
         dp_copy(lax.rem(q + k, n_dp), q).start()
         return c
 
-    lax.fori_loop(1, n_dp, send_dp, 0)
+    def send_lo(k, c):
+        dp_copy(row * n_lo + lax.rem(lo + k, n_lo), q).start()
+        return c
+
+    own_dp = pltpu.make_async_copy(dp_send if bcast else dp_send.at[q], dp_recv.at[q], own_sems.at[1])
+    if bcast:
+        lax.fori_loop(1, n_lo, send_lo, 0)
+    else:
+        lax.fori_loop(1, n_dp, send_dp, 0)
+    own_dp.start()
     lax.fori_loop(1, n_ex, send_ex, 0)
     own_ex = pltpu.make_async_copy(ex_send.at[p], ex_recv.at[p], own_sems.at[0])
-    own_dp = pltpu.make_async_copy(dp_send if bcast else dp_send.at[q], dp_recv.at[q], own_sems.at[1])
     own_ex.start()
-    own_dp.start()
 
     def wait_ex(k, c):
         j = lax.rem(p + k, n_ex)
@@ -67,18 +84,42 @@
         dp_copy(i, i).wait_recv()
         return c
 
-    lax.fori_loop(1, n_ex, wait_ex, 0)
-    lax.fori_loop(1, n_dp, wait_dp, 0)
+    def wait_lo(k, c):
+        i = row * n_lo + lax.rem(lo + k, n_lo)
+        dp_copy(i, q).wait_send()
+        dp_copy(i, i).wait_recv()
+        return c
+
+    def send_hi(k, c):
+        row_copy(lax.rem(row + k, n_hi), row, k).start()
+        return c
+
+    def wait_hi(k, c):
+        r = lax.rem(row + k, n_hi)
+        row_copy(r, row, k).wait_send()
+        row_copy(r, r, k).wait_recv()
+        return c
+
+    if bcast:
+        lax.fori_loop(1, n_lo, wait_lo, 0)
+        own_dp.wait()
+        lax.fori_loop(1, n_hi, send_hi, 0)
+        lax.fori_loop(1, n_ex, wait_ex, 0)
+        lax.fori_loop(1, n_hi, wait_hi, 0)
+    else:
+        lax.fori_loop(1, n_ex, wait_ex, 0)
+        lax.fori_loop(1, n_dp, wait_dp, 0)
+        own_dp.wait()
     own_ex.wait()
-    own_dp.wait()
 
 
 def exchange(ex_send, dp_send, bcast, cid):
     n_dp = lax.axis_size("dp")
     n_ex = lax.axis_size("expert")
     dp_block = dp_send.shape if bcast else dp_send.shape[1:]
+    n_lo = 4 if n_dp % 4 == 0 else n_dp
     return pl.pallas_call(
-        functools.partial(exchange_kernel, n_dp, n_ex, bcast),
+        functools.partial(exchange_kernel, n_dp, n_ex, n_lo, bcast),
         out_shape=(
             jax.ShapeDtypeStruct(ex_send.shape, ex_send.dtype),
             jax.ShapeDtypeStruct((n_dp,) + tuple(dp_block), dp_send.dtype),
@@ -86,8 +127,8 @@
         in_specs=[pl.BlockSpec(memory_space=pl.ANY)] * 2,
         out_specs=(pl.BlockSpec(memory_space=pl.ANY), pl.BlockSpec(memory_space=pl.ANY)),
         scratch_shapes=[
-            pltpu.SemaphoreType.DMA((n_ex + n_dp,)),
-            pltpu.SemaphoreType.DMA((n_ex + n_dp,)),
+            pltpu.SemaphoreType.DMA((n_ex + n_dp + n_dp,)),
+            pltpu.SemaphoreType.DMA((n_ex + n_dp + n_dp,)),
             pltpu.SemaphoreType.DMA((2,)),
         ],
         compiler_params=pltpu.CompilerParams(collective_id=cid, has_side_effects=True),

time: 743 us -> 665 us (0.90)
  the two profiles are of different devices: /device:TPU:39 before, /device:TPU:33 now
where the time goes in v3:
time: 665 us
  Pallas kernels  593 us (89%)
  local copies, waits for them, and re-layouts  36.7 us (6%)
  other arithmetic  21.3 us (3%)
  matrix products  13 us (2%)
    pallas_call x2, Pallas kernels, exchange(): pl.pallas_call(functools.partial(exchange_kernel, n_dp, n_ex, n_lo, bcast...  593 us

profile of v3, /device:TPU:33, one launch (start us, length us, event | category | flops | bytes accessed | tf_op | source)
XLA Modules:
  0.0 664.7 jit_solution(14810092834641177228)
XLA Ops:
  0.6 0.0 copy-start
  0.6 0.8 copy.17
  1.5 0.1 eq.39
  1.6 0.6 reduce-window.6
  2.2 0.2 slice_reduce_fusion
  2.5 0.1 reshape.194
  2.6 0.1 fusion.24
  2.7 0.2 select_reduce_fusion
  2.9 0.8 copy.16
  3.7 0.1 reshape.196
  3.9 2.5 gather_fusion.1
  6.3 0.1 gather.24
  6.4 0.2 fusion.21
  6.6 0.1 broadcast_in_dim.42
  6.7 0.0 copy-done
  6.7 2.4 gather_fusion.2
  9.2 2.1 reshape.202
  11.3 0.0 copy-start.2
  11.3 3.9 multiply_convert_fusion.1
  15.2 0.0 copy-done.2
  15.2 3.0 gather_fusion
  18.1 1.6 gather.22
  19.7 0.0 copy-start.3
  19.7 0.2 broadcast_select_fusion
  19.9 1.4 copy-done.3
  21.3 0.0 copy-start.4
  21.3 0.0 copy-start.5
  21.3 2.9 pad_maximum_fusion.ex_send
  24.1 0.0 copy-done.4
  24.1 0.0 copy-done.5
  24.1 0.9 pad_maximum_fusion.2.dp_send
  25.0 331.7 %shard_map.85 = (bf16[32,9,4096]{2,1,0:T(8,128)(2,1)}, bf16[16,128,2304]{2,1,0:T(8,128)(2,1)}) custom-call(bf16[32,9,4096]{2,1,0:T(8,128)(2,1)} %pad_maximum_fusion.ex_send, bf16[128,2304]{1,0:T(8,128)(2,1)} %pad_maximum_fusion.2.dp_send), custom_call_target="tpu_custom_call" | custom-call | tf_op jit(solution)/shard_map/pallas_call | solution.py:121
  356.7 3.4 reshape.197
  360.1 0.0 copy-start.7
  360.1 4.9 fusion.2
  365.0 0.6 copy-done.7
  365.6 1.4 multiply_convert_fusion.3
  367.0 3.6 multiply_convert_fusion
  370.6 1.1 fusion.11
  371.7 2.0 fusion.8
  373.7 0.2 pad_maximum_fusion.1
  373.9 2.8 reshape.199.ex_send
  376.7 261.0 %shard_map.86 = (bf16[32,9,4096]{2,1,0:T(8,128)(2,1)}, bf16[16,128,768]{2,1,0:T(8,128)(2,1)}) custom-call(bf16[32,9,4096]{2,1,0:T(8,128)(2,1)} %reshape.199.ex_send, bf16[16,128,768]{2,1,0:T(8,128)(2,1)} %bitcast.28), custom_call_target="tpu_custom_call" | custom-call | tf_op jit(solution)/shard_map/pallas_call | solution.py:121
  637.8 4.7 reshape.201
  642.5 0.0 copy-start.6
  642.5 1.8 fusion.29
  644.3 0.0 copy-done.6
  644.3 0.1 copy.21
  644.4 0.1 mul.89
  644.6 2.3 gather_fusion.3
  646.9 3.4 reshape.203
  650.3 5.6 multiply_reduce_fusion
  655.9 1.4 gather_fusion.4
  657.2 0.0 copy-start.1
  657.3 0.7 gather.28
  658.0 3.6 reduce_sum.60
  661.6 3.0 reduce_sum.61
  664.7 0.0 copy-done.1
  (10 shorter events, 0.1 us)
Async XLA Ops:
  0.6 6.1 copy-start
  11.3 3.9 copy-start.2
  19.7 1.6 copy-start.3
  21.3 2.9 copy-start.4
  21.3 2.9 copy-start.5
  360.1 5.5 copy-start.7
  642.5 1.8 copy-start.6
  657.2 7.4 %copy-start.1 = (bf16[128,2048]{1,0:T(8,128)(2,1)S(1)}, bf16[128,2048]{1,0:T(8,128)(2,1)}, u32[]{:S(2)}) copy-start(bf16[128,2048]{1,0:T(8,128)(2,1)} %param.7) | copy-start | bytes 1572868

commit v4 on v3

--- a/solution.py
+++ b/solution.py
@@ -19,9 +19,17 @@
     row = q // n_lo
     lo = q % n_lo
     barrier = pltpu.get_barrier_semaphore()
+    far = n_lo == 4 and n_ex % 8 == 0
+
+    def peer_q(j):
+        if not far:
+            return q
+        gap = lax.rem(j // 2 - p // 2 + 8 * n_ex, 4)
+        return q + (gap // 2) * (1 - gap % 2) * (3 - 2 * lo)
 
     def greet_ex(k, c):
-        pl.semaphore_signal(barrier, 1, device_id=(q, lax.rem(p + k, n_ex)), device_id_type=MESH)
+        j = lax.rem(p + k, n_ex)
+        pl.semaphore_signal(barrier, 1, device_id=(peer_q(j), j), device_id_type=MESH)
         return c
 
     def greet_dp(k, c):
@@ -35,7 +43,7 @@
     def ex_copy(j, slot):
         return pltpu.make_async_remote_copy(
             src_ref=ex_send.at[j], dst_ref=ex_recv.at[slot], send_sem=send_sems.at[j],
-            recv_sem=recv_sems.at[slot], device_id=(q, j), device_id_type=MESH)
+            recv_sem=recv_sems.at[slot], device_id=(peer_q(j), j), device_id_type=MESH)
 
     def dp_copy(i, slot):
         src = dp_send if bcast else dp_send.at[i]

time: 665 us -> 605 us (0.910)
  the two profiles are of different devices: /device:TPU:33 before, /device:TPU:15 now
where the time goes in v4:
time: 605 us; the launch traced here: 604 us
  Pallas kernels  532 us (88%)
  local copies, waits for them, and re-layouts  36.7 us (6%)
  other arithmetic  21.3 us (4%)
  matrix products  13 us (2%)
    pallas_call x2, Pallas kernels, exchange(): pl.pallas_call(functools.partial(exchange_kernel, n_dp, n_ex, n_lo, bcast...  532 us

profile of v4, /device:TPU:15, one launch (start us, length us, event | category | flops | bytes accessed | tf_op | source)
XLA Modules:
  0.0 604.1 jit_solution(1089302869865061425)
XLA Ops:
  0.6 0.0 copy-start
  0.6 0.8 copy.17
  1.5 0.1 eq.39
  1.6 0.6 reduce-window.6
  2.2 0.2 slice_reduce_fusion
  2.5 0.1 reshape.194
  2.6 0.1 fusion.24
  2.7 0.2 select_reduce_fusion
  2.9 0.8 copy.16
  3.7 0.1 reshape.196
  3.9 2.5 gather_fusion.1
  6.3 0.1 gather.24
  6.4 0.2 fusion.21
  6.6 0.1 broadcast_in_dim.42
  6.7 0.0 copy-done
  6.7 2.4 gather_fusion.2
  9.2 2.1 reshape.202
  11.3 0.0 copy-start.2
  11.3 3.9 multiply_convert_fusion.1
  15.2 0.0 copy-done.2
  15.2 3.0 gather_fusion
  18.1 1.6 gather.22
  19.7 0.0 copy-start.3
  19.7 0.2 broadcast_select_fusion
  19.9 1.4 copy-done.3
  21.3 0.0 copy-start.4
  21.3 0.0 copy-start.5
  21.3 2.9 pad_maximum_fusion.ex_send
  24.1 0.0 copy-done.4
  24.1 0.0 copy-done.5
  24.1 0.9 pad_maximum_fusion.2.dp_send
  25.0 259.0 %shard_map.85 = (bf16[32,9,4096]{2,1,0:T(8,128)(2,1)}, bf16[16,128,2304]{2,1,0:T(8,128)(2,1)}) custom-call(bf16[32,9,4096]{2,1,0:T(8,128)(2,1)} %pad_maximum_fusion.ex_send, bf16[128,2304]{1,0:T(8,128)(2,1)} %pad_maximum_fusion.2.dp_send), custom_call_target="tpu_custom_call" | custom-call | tf_op jit(solution)/shard_map/pallas_call | solution.py:129
  284.0 3.4 reshape.197
  287.4 0.0 copy-start.7
  287.4 4.9 fusion.2
  292.3 0.6 copy-done.7
  292.9 1.4 multiply_convert_fusion.3
  294.3 3.6 multiply_convert_fusion
  297.9 1.1 fusion.11
  299.0 2.0 fusion.8
  301.0 0.2 pad_maximum_fusion.1
  301.2 2.8 reshape.199.ex_send
  304.0 273.2 %shard_map.86 = (bf16[32,9,4096]{2,1,0:T(8,128)(2,1)}, bf16[16,128,768]{2,1,0:T(8,128)(2,1)}) custom-call(bf16[32,9,4096]{2,1,0:T(8,128)(2,1)} %reshape.199.ex_send, bf16[16,128,768]{2,1,0:T(8,128)(2,1)} %bitcast.28), custom_call_target="tpu_custom_call" | custom-call | tf_op jit(solution)/shard_map/pallas_call | solution.py:129
  577.2 4.7 reshape.201
  581.9 0.0 copy-start.6
  581.9 1.8 fusion.29
  583.7 0.0 copy-done.6
  583.8 0.1 copy.21
  583.9 0.1 mul.89
  584.0 2.3 gather_fusion.3
  586.4 3.4 reshape.203
  589.8 5.6 multiply_reduce_fusion
  595.4 1.4 gather_fusion.4
  596.7 0.0 copy-start.1
  596.7 0.7 gather.28
  597.5 3.6 reduce_sum.60
  601.1 3.0 reduce_sum.61
  604.1 0.0 copy-done.1
  (10 shorter events, 0.1 us)
Async XLA Ops:
  0.6 6.1 %copy-start = (bf16[128,2048]{1,0:T(8,128)(2,1)S(1)}, bf16[128,2048]{1,0:T(8,128)(2,1)}, u32[]{:S(2)}) copy-start(bf16[128,2048]{1,0:T(8,128)(2,1)} %param.7) | copy-start | bytes 1572868
  11.3 3.9 copy-start.2
  19.7 1.6 copy-start.3
  21.3 2.9 copy-start.4
  21.3 2.9 copy-start.5
  287.4 5.5 copy-start.7
  581.9 1.8 copy-start.6
  596.7 7.4 %copy-start.1 = (bf16[128,2048]{1,0:T(8,128)(2,1)S(1)}, bf16[128,2048]{1,0:T(8,128)(2,1)}, u32[]{:S(2)}) copy-start(bf16[128,2048]{1,0:T(8,128)(2,1)} %param.7) | copy-start | bytes 1572868

commit v5 on v4

--- a/solution.py
+++ b/solution.py
@@ -190,7 +190,7 @@
     send_grad = (weight_slot[:, None] * out_grad[token_of_slot].astype(jnp.float32)).astype(
         jnp.bfloat16
     )
-    block_shape = (peer_count, local_count * capacity, 2 * model_width)
+    block_shape = (peer_count, local_count * capacity * 2 * model_width // 128, 128)
     send_both = jnp.concatenate([send_rows, send_grad], axis=1).reshape(block_shape)
     gate_width = gate_up_weight.shape[2]
     joined = jnp.concatenate([gate_up_weight[0], down_weight[0]], axis=1)

time: 605 us -> 455 us (0.75)
  the two profiles are of different devices: /device:TPU:15 before, /device:TPU:95 now
where the time goes in v5:
time: 455 us; the launch traced here: 454 us
  Pallas kernels  388 us (85%)
  local copies, waits for them, and re-layouts  34.3 us (8%)
  other arithmetic  16.1 us (4%)
  matrix products  15 us (3%)
    pallas_call x2, Pallas kernels, exchange(): pl.pallas_call(functools.partial(exchange_kernel, n_dp, n_ex, n_lo, bcast...  388 us

profile of v5, /device:TPU:95, one launch (start us, length us, event | category | flops | bytes accessed | tf_op | source)
XLA Modules:
  0.0 454.1 jit_solution(13395472960252666625)
XLA Ops:
  0.6 0.0 copy-start
  0.6 0.8 copy.17
  1.5 0.1 reshape.178
  1.6 0.1 eq.39
  1.8 0.6 reduce-window.6
  2.4 0.2 slice_reduce_fusion
  2.6 0.1 fusion.24
  2.7 0.2 select_reduce_fusion
  2.9 0.0 copy-done
  2.9 0.0 copy-start.7
  2.9 2.4 gather_fusion.2
  5.4 0.0 copy-start.1
  5.4 0.1 fusion.21
  5.6 0.0 copy-done.7
  5.6 0.1 copy.16
  5.7 0.1 reshape.180
  5.8 2.5 gather_fusion.1
  8.3 1.3 multiply_convert_fusion.1
  9.6 0.0 copy-done.1
  9.6 2.4 gather_fusion
  12.0 0.0 copy-start.2
  12.0 0.1 broadcast_select_fusion
  12.2 1.1 copy-done.2
  13.3 0.2 pad_maximum_fusion
  13.5 0.0 copy-start.4
  13.5 0.0 copy-start.5
  13.5 2.5 reshape.181.ex_send
  16.0 0.0 copy-done.4
  16.0 0.0 copy-done.5
  16.0 0.8 pad_maximum_fusion.2.dp_send
  16.9 227.7 %shard_map.85 = (bf16[32,288,128]{2,1,0:T(8,128)(2,1)}, bf16[16,128,2304]{2,1,0:T(8,128)(2,1)}) custom-call(bf16[32,288,128]{2,1,0:T(8,128)(2,1)} %reshape.181.ex_send, bf16[128,2304]{1,0:T(8,128)(2,1)} %pad_maximum_fusion.2.dp_send), custom_call_target="tpu_custom_call" | custom-call | tf_op jit(solution)/shard_map/pallas_call | solution.py:129
  244.6 3.7 reshape.182
  248.2 0.0 copy-start.3
  248.2 0.0 copy-start.8
  248.3 5.7 %fusion.2 = f32[288,1536]{1,0:T(8,128)S(1)} fusion(bf16[2048,2304]{1,0:T(8,128)(2,1)} %bitcast.34, bf16[288,4096]{1,0:T(8,128)(2,1)S(1)} %reshape.182), kind=kOutput, calls=%fused_computation.8 | convolution fusion | flops 1811939328 | bytes 9240576 | tf_op jit(solution)/shard_map/dot_general | solution.py:147
  253.9 0.0 copy-done.3
  253.9 0.7 copy-done.8
  254.6 1.4 multiply_convert_fusion.3
  256.0 2.0 fusion.8
  258.0 1.1 fusion.11
  259.1 0.2 pad_maximum_fusion.1
  259.3 2.5 reshape.184.ex_send
  261.9 4.8 %multiply_convert_fusion = bf16[2048,768]{1,0:T(8,128)(2,1)} fusion(bf16[288,768]{1,0:T(8,128)(2,1)S(1)} %get-tuple-element.17, bf16[288,4096]{1,0:T(8,128)(2,1)} %copy-done.3), kind=kOutput, calls=%fused_computation.5 | convolution fusion | flops 909115392 | bytes 4767744 | tf_op jit(solution)/shard_map/dot_general | solution.py:158
  266.7 160.1 %shard_map.86 = (bf16[32,288,128]{2,1,0:T(8,128)(2,1)}, bf16[16,128,768]{2,1,0:T(8,128)(2,1)}) custom-call(bf16[32,288,128]{2,1,0:T(8,128)(2,1)} %reshape.184.ex_send, bf16[16,128,768]{2,1,0:T(8,128)(2,1)} %bitcast.28), custom_call_target="tpu_custom_call" | custom-call | tf_op jit(solution)/shard_map/pallas_call | solution.py:129
  426.8 5.1 %reshape.186 = bf16[288,4096]{1,0:T(8,128)(2,1)} reshape(bf16[32,288,128]{2,1,0:T(8,128)(2,1)} %get-tuple-element.9) | data formatting | bytes 4718592 | tf_op jit(solution)/shard_map/reshape | solution.py:224
  431.9 0.0 copy-start.6
  431.9 1.8 fusion.29
  433.7 0.0 copy-done.6
  433.8 0.1 copy.21
  433.9 0.1 mul.88
  434.1 2.4 gather_fusion.3
  436.4 3.3 reshape.187
  439.8 5.6 %multiply_reduce_fusion = bf16[128,2048]{1,0:T(8,128)(2,1)} fusion(f32[128,2,2048]{2,1,0:T(2,128)} %reshape.187, f32[128,2]{1,0:T(8,128)S(1)} %copy.16), kind=kLoop, calls=%fused_computation.19 | loop fusion | flops 786432 | bytes 2622464 | tf_op jit(solution)/shard_map/reduce_sum | solution.py:228
  445.3 1.4 gather_fusion.4
  446.7 0.7 gather.22
  447.4 3.6 reduce_sum.60
  451.1 3.0 reduce_sum.61
  (10 shorter events, 0.1 us)
Async XLA Ops:
  0.6 2.3 copy-start
  2.9 2.6 copy-start.7
  5.4 4.2 copy-start.1
  12.0 1.3 copy-start.2
  13.5 2.5 copy-start.4
  13.5 2.5 copy-start.5
  248.2 5.7 %copy-start.3 = (bf16[288,4096]{1,0:T(8,128)(2,1)}, bf16[288,4096]{1,0:T(8,128)(2,1)S(1)}, u32[]{:S(2)}) copy-start(bf16[288,4096]{1,0:T(8,128)(2,1)S(1)} %reshape.182) | copy-start | bytes 7077892
  248.2 6.3 %copy-start.8 = (bf16[16,128,2304]{2,1,0:T(8,128)(2,1)S(1)}, bf16[16,128,2304]{2,1,0:T(8,128)(2,1)}, u32[]{:S(2)}) copy-start(bf16[16,128,2304]{2,1,0:T(8,128)(2,1)} %get-tuple-element.8) | copy-start | bytes 28311556
  431.9 1.8 copy-start.6

commit v6 on v5

--- a/solution.py
+++ b/solution.py
@@ -108,7 +108,38 @@
         row_copy(r, r, k).wait_recv()
         return c
 
-    if bcast:
+    def fwd_copy(start, count, target_row, s_idx, r_idx):
+        rows = dp_recv.at[pl.ds(start, count)]
+        return pltpu.make_async_remote_copy(
+            src_ref=rows, dst_ref=rows, send_sem=send_sems.at[n_ex + n_dp + s_idx],
+            recv_sem=recv_sems.at[n_ex + n_dp + r_idx],
+            device_id=(target_row * n_lo + lo, p), device_id_type=MESH)
+
+    if bcast and n_hi == 4:
+        half = n_lo // 2
+        up = lax.rem(row + 1, 4)
+        dn = lax.rem(row + 3, 4)
+        far_row = lax.rem(row + 2, 4)
+        lax.fori_loop(1, n_lo, wait_lo, 0)
+        own_dp.wait()
+        to_up = fwd_copy(row * n_lo, n_lo, up, 0, row)
+        to_dn = fwd_copy(row * n_lo, n_lo, dn, 1, row)
+        to_up.start()
+        to_dn.start()
+        fwd_copy(dn * n_lo, n_lo, dn, 0, dn).wait_recv()
+        fwd_copy(up * n_lo, n_lo, up, 1, up).wait_recv()
+        pass_up = fwd_copy(dn * n_lo, half, up, 2, 4)
+        pass_dn = fwd_copy(up * n_lo + half, n_lo - half, dn, 3, 5)
+        pass_up.start()
+        pass_dn.start()
+        lax.fori_loop(1, n_ex, wait_ex, 0)
+        fwd_copy(far_row * n_lo, half, up, 2, 4).wait_recv()
+        fwd_copy(far_row * n_lo + half, n_lo - half, dn, 3, 5).wait_recv()
+        to_up.wait_send()
+        to_dn.wait_send()
+        pass_up.wait_send()
+        pass_dn.wait_send()
+    elif bcast:
         lax.fori_loop(1, n_lo, wait_lo, 0)
         own_dp.wait()
         lax.fori_loop(1, n_hi, send_hi, 0)

time: 455 us -> 431 us (0.947)
  the two profiles are of different devices: /device:TPU:95 before, /device:TPU:67 now
where the time goes in v6:
time: 431 us; the launch traced here: 430 us
  Pallas kernels  364 us (84%)
  local copies, waits for them, and re-layouts  34.3 us (8%)
  other arithmetic  16.1 us (4%)
  matrix products  15 us (3%)
    pallas_call x2, Pallas kernels, exchange(): pl.pallas_call(functools.partial(exchange_kernel, n_dp, n_ex, n_lo, bcast...  364 us

profile of v6, /device:TPU:67, one launch (start us, length us, event | category | flops | bytes accessed | tf_op | source)
XLA Modules:
  0.0 430.5 jit_solution(494097748571041915)
XLA Ops:
  0.6 0.0 copy-start
  0.6 0.8 copy.17
  1.5 0.1 reshape.178
  1.6 0.1 eq.39
  1.8 0.6 reduce-window.6
  2.4 0.2 slice_reduce_fusion
  2.6 0.1 fusion.24
  2.7 0.2 select_reduce_fusion
  2.9 0.0 copy-done
  2.9 0.0 copy-start.7
  2.9 2.4 gather_fusion.2
  5.4 0.0 copy-start.1
  5.4 0.1 fusion.21
  5.6 0.0 copy-done.7
  5.6 0.1 copy.16
  5.7 0.1 reshape.180
  5.8 2.5 gather_fusion.1
  8.3 1.3 multiply_convert_fusion.1
  9.6 0.0 copy-done.1
  9.6 2.4 gather_fusion
  12.0 0.0 copy-start.2
  12.0 0.1 broadcast_select_fusion
  12.2 1.1 copy-done.2
  13.3 0.2 pad_maximum_fusion
  13.5 0.0 copy-start.4
  13.5 0.0 copy-start.5
  13.5 2.5 reshape.181.ex_send
  16.0 0.0 copy-done.4
  16.0 0.0 copy-done.5
  16.0 0.8 pad_maximum_fusion.2.dp_send
  16.9 205.4 %shard_map.85 = (bf16[32,288,128]{2,1,0:T(8,128)(2,1)}, bf16[16,128,2304]{2,1,0:T(8,128)(2,1)}) custom-call(bf16[32,288,128]{2,1,0:T(8,128)(2,1)} %reshape.181.ex_send, bf16[128,2304]{1,0:T(8,128)(2,1)} %pad_maximum_fusion.2.dp_send), custom_call_target="tpu_custom_call" | custom-call | tf_op jit(solution)/shard_map/pallas_call | solution.py:160
  222.3 3.7 reshape.182
  226.0 0.0 copy-start.3
  226.0 0.0 copy-start.8
  226.0 5.7 %fusion.2 = f32[288,1536]{1,0:T(8,128)S(1)} fusion(bf16[2048,2304]{1,0:T(8,128)(2,1)} %bitcast.34, bf16[288,4096]{1,0:T(8,128)(2,1)S(1)} %reshape.182), kind=kOutput, calls=%fused_computation.8 | convolution fusion | flops 1811939328 | bytes 9240576 | tf_op jit(solution)/shard_map/dot_general | solution.py:178
  231.6 0.0 copy-done.3
  231.6 0.7 copy-done.8
  232.3 1.4 multiply_convert_fusion.3
  233.7 2.0 fusion.8
  235.7 1.1 fusion.11
  236.8 0.2 pad_maximum_fusion.1
  237.0 2.5 reshape.184.ex_send
  239.6 4.8 %multiply_convert_fusion = bf16[2048,768]{1,0:T(8,128)(2,1)} fusion(bf16[288,768]{1,0:T(8,128)(2,1)S(1)} %get-tuple-element.17, bf16[288,4096]{1,0:T(8,128)(2,1)} %copy-done.3), kind=kOutput, calls=%fused_computation.5 | convolution fusion | flops 909115392 | bytes 4767744 | tf_op jit(solution)/shard_map/dot_general | solution.py:189
  244.4 158.8 %shard_map.86 = (bf16[32,288,128]{2,1,0:T(8,128)(2,1)}, bf16[16,128,768]{2,1,0:T(8,128)(2,1)}) custom-call(bf16[32,288,128]{2,1,0:T(8,128)(2,1)} %reshape.184.ex_send, bf16[16,128,768]{2,1,0:T(8,128)(2,1)} %bitcast.28), custom_call_target="tpu_custom_call" | custom-call | tf_op jit(solution)/shard_map/pallas_call | solution.py:160
  403.2 5.1 %reshape.186 = bf16[288,4096]{1,0:T(8,128)(2,1)} reshape(bf16[32,288,128]{2,1,0:T(8,128)(2,1)} %get-tuple-element.9) | data formatting | bytes 4718592 | tf_op jit(solution)/shard_map/reshape | solution.py:255
  408.3 0.0 copy-start.6
  408.3 1.8 fusion.29
  410.1 0.0 copy-done.6
  410.1 0.1 copy.21
  410.3 0.1 mul.88
  410.4 2.4 gather_fusion.3
  412.8 3.3 reshape.187
  416.1 5.6 %multiply_reduce_fusion = bf16[128,2048]{1,0:T(8,128)(2,1)} fusion(f32[128,2,2048]{2,1,0:T(2,128)} %reshape.187, f32[128,2]{1,0:T(8,128)S(1)} %copy.16), kind=kLoop, calls=%fused_computation.19 | loop fusion | flops 786432 | bytes 2622464 | tf_op jit(solution)/shard_map/reduce_sum | solution.py:259
  421.7 1.4 gather_fusion.4
  423.1 0.7 gather.22
  423.8 3.6 reduce_sum.60
  427.4 3.0 reduce_sum.61
  (10 shorter events, 0.1 us)
Async XLA Ops:
  0.6 2.3 copy-start
  2.9 2.6 copy-start.7
  5.4 4.2 copy-start.1
  12.0 1.3 copy-start.2
  13.5 2.5 copy-start.4
  13.5 2.5 copy-start.5
  226.0 5.7 %copy-start.3 = (bf16[288,4096]{1,0:T(8,128)(2,1)}, bf16[288,4096]{1,0:T(8,128)(2,1)S(1)}, u32[]{:S(2)}) copy-start(bf16[288,4096]{1,0:T(8,128)(2,1)S(1)} %reshape.182) | copy-start | bytes 7077892
  226.0 6.3 %copy-start.8 = (bf16[16,128,2304]{2,1,0:T(8,128)(2,1)S(1)}, bf16[16,128,2304]{2,1,0:T(8,128)(2,1)}, u32[]{:S(2)}) copy-start(bf16[16,128,2304]{2,1,0:T(8,128)(2,1)} %get-tuple-element.8) | copy-start | bytes 28311556
  408.3 1.8 copy-start.6

commit v7 on v6

--- a/solution.py
+++ b/solution.py
@@ -76,9 +76,11 @@
     else:
         lax.fori_loop(1, n_dp, send_dp, 0)
     own_dp.start()
-    lax.fori_loop(1, n_ex, send_ex, 0)
     own_ex = pltpu.make_async_copy(ex_send.at[p], ex_recv.at[p], own_sems.at[0])
     own_ex.start()
+    late = bcast and n_hi == 4
+    if not late:
+        lax.fori_loop(1, n_ex, send_ex, 0)
 
     def wait_ex(k, c):
         j = lax.rem(p + k, n_ex)
@@ -126,6 +128,7 @@
         to_dn = fwd_copy(row * n_lo, n_lo, dn, 1, row)
         to_up.start()
         to_dn.start()
+        lax.fori_loop(1, n_ex, send_ex, 0)
         fwd_copy(dn * n_lo, n_lo, dn, 0, dn).wait_recv()
         fwd_copy(up * n_lo, n_lo, up, 1, up).wait_recv()
         pass_up = fwd_copy(dn * n_lo, half, up, 2, 4)

time: 431 us -> 406 us (0.942)
  the two profiles are of different devices: /device:TPU:67 before, /device:TPU:75 now
where the time goes in v7:
time: 406 us
  Pallas kernels  340 us (84%)
  local copies, waits for them, and re-layouts  34.3 us (8%)
  other arithmetic  16.1 us (4%)
  matrix products  15 us (4%)
    pallas_call x2, Pallas kernels, exchange(): pl.pallas_call(functools.partial(exchange_kernel, n_dp, n_ex, n_lo, bcast...  340 us

profile of v7, /device:TPU:75, one launch (start us, length us, event | category | flops | bytes accessed | tf_op | source)
XLA Modules:
  0.0 406.0 jit_solution(3767904710869823245)
XLA Ops:
  0.6 0.0 copy-start
  0.6 0.8 copy.17
  1.5 0.1 reshape.178
  1.6 0.1 eq.39
  1.8 0.6 reduce-window.6
  2.4 0.2 slice_reduce_fusion
  2.6 0.1 fusion.24
  2.7 0.2 select_reduce_fusion
  2.9 0.0 copy-done
  2.9 0.0 copy-start.7
  2.9 2.4 gather_fusion.2
  5.4 0.0 copy-start.1
  5.4 0.1 fusion.21
  5.6 0.0 copy-done.7
  5.6 0.1 copy.16
  5.7 0.1 reshape.180
  5.8 2.5 gather_fusion.1
  8.3 1.3 multiply_convert_fusion.1
  9.6 0.0 copy-done.1
  9.6 2.4 gather_fusion
  12.0 0.0 copy-start.2
  12.0 0.1 broadcast_select_fusion
  12.2 1.1 copy-done.2
  13.3 0.2 pad_maximum_fusion
  13.5 0.0 copy-start.4
  13.5 0.0 copy-start.5
  13.5 2.5 reshape.181.ex_send
  16.0 0.0 copy-done.4
  16.0 0.0 copy-done.5
  16.0 0.8 pad_maximum_fusion.2.dp_send
  16.9 159.6 %shard_map.85 = (bf16[32,288,128]{2,1,0:T(8,128)(2,1)}, bf16[16,128,2304]{2,1,0:T(8,128)(2,1)}) custom-call(bf16[32,288,128]{2,1,0:T(8,128)(2,1)} %reshape.181.ex_send, bf16[128,2304]{1,0:T(8,128)(2,1)} %pad_maximum_fusion.2.dp_send), custom_call_target="tpu_custom_call" | custom-call | tf_op jit(solution)/shard_map/pallas_call | solution.py:163
  176.5 3.7 reshape.182
  180.2 0.0 copy-start.3
  180.2 0.0 copy-start.8
  180.2 5.7 %fusion.2 = f32[288,1536]{1,0:T(8,128)S(1)} fusion(bf16[2048,2304]{1,0:T(8,128)(2,1)} %bitcast.34, bf16[288,4096]{1,0:T(8,128)(2,1)S(1)} %reshape.182), kind=kOutput, calls=%fused_computation.8 | convolution fusion | flops 1811939328 | bytes 9240576 | tf_op jit(solution)/shard_map/dot_general | solution.py:181
  185.8 0.0 copy-done.3
  185.9 0.7 copy-done.8
  186.5 1.4 multiply_convert_fusion.3
  187.9 2.0 fusion.8
  189.9 1.1 fusion.11
  191.1 0.2 pad_maximum_fusion.1
  191.3 2.5 reshape.184.ex_send
  193.8 4.8 %multiply_convert_fusion = bf16[2048,768]{1,0:T(8,128)(2,1)} fusion(bf16[288,768]{1,0:T(8,128)(2,1)S(1)} %get-tuple-element.17, bf16[288,4096]{1,0:T(8,128)(2,1)} %copy-done.3), kind=kOutput, calls=%fused_computation.5 | convolution fusion | flops 909115392 | bytes 4767744 | tf_op jit(solution)/shard_map/dot_general | solution.py:192
  198.6 180.0 %shard_map.86 = (bf16[32,288,128]{2,1,0:T(8,128)(2,1)}, bf16[16,128,768]{2,1,0:T(8,128)(2,1)}) custom-call(bf16[32,288,128]{2,1,0:T(8,128)(2,1)} %reshape.184.ex_send, bf16[16,128,768]{2,1,0:T(8,128)(2,1)} %bitcast.28), custom_call_target="tpu_custom_call" | custom-call | tf_op jit(solution)/shard_map/pallas_call | solution.py:163
  378.7 5.1 %reshape.186 = bf16[288,4096]{1,0:T(8,128)(2,1)} reshape(bf16[32,288,128]{2,1,0:T(8,128)(2,1)} %get-tuple-element.9) | data formatting | bytes 4718592 | tf_op jit(solution)/shard_map/reshape | solution.py:258
  383.8 0.0 copy-start.6
  383.8 1.8 fusion.29
  385.6 0.0 copy-done.6
  385.6 0.1 copy.21
  385.7 0.1 mul.88
  385.9 2.4 gather_fusion.3
  388.3 3.3 reshape.187
  391.6 5.6 %multiply_reduce_fusion = bf16[128,2048]{1,0:T(8,128)(2,1)} fusion(f32[128,2,2048]{2,1,0:T(2,128)} %reshape.187, f32[128,2]{1,0:T(8,128)S(1)} %copy.16), kind=kLoop, calls=%fused_computation.19 | loop fusion | flops 786432 | bytes 2622464 | tf_op jit(solution)/shard_map/reduce_sum | solution.py:262
  397.2 1.4 gather_fusion.4
  398.5 0.7 gather.22
  399.3 3.6 reduce_sum.60
  402.9 3.0 reduce_sum.61
  (10 shorter events, 0.1 us)
Async XLA Ops:
  0.6 2.3 copy-start
  2.9 2.6 copy-start.7
  5.4 4.2 %copy-start.1 = (bf16[128,2048]{1,0:T(8,128)(2,1)S(1)}, bf16[128,2048]{1,0:T(8,128)(2,1)}, u32[]{:S(2)}) copy-start(bf16[128,2048]{1,0:T(8,128)(2,1)} %param.6) | copy-start | bytes 1572868
  12.0 1.3 copy-start.2
  13.5 2.5 copy-start.4
  13.5 2.5 copy-start.5
  180.2 5.7 %copy-start.3 = (bf16[288,4096]{1,0:T(8,128)(2,1)}, bf16[288,4096]{1,0:T(8,128)(2,1)S(1)}, u32[]{:S(2)}) copy-start(bf16[288,4096]{1,0:T(8,128)(2,1)S(1)} %reshape.182) | copy-start | bytes 7077892
  180.2 6.3 %copy-start.8 = (bf16[16,128,2304]{2,1,0:T(8,128)(2,1)S(1)}, bf16[16,128,2304]{2,1,0:T(8,128)(2,1)}, u32[]{:S(2)}) copy-start(bf16[16,128,2304]{2,1,0:T(8,128)(2,1)} %get-tuple-element.8) | copy-start | bytes 28311556
  383.8 1.8 copy-start.6

commit v8 on v7

--- a/solution.py
+++ b/solution.py
@@ -255,10 +255,11 @@
         [produced.astype(jnp.bfloat16), input_grad.astype(jnp.bfloat16)], axis=1
     ).reshape(block_shape)
     returned, down_recv = exchange(back_both, down_parts, False, 1)
-    returned = returned.reshape(slot_count, 2 * model_width)
-    out_pairs = returned[:, :model_width][slot_of_pair]
-    grad_pairs = returned[:, model_width:][slot_of_pair]
-    weighted = probs_flat[:, None] * out_pairs.astype(jnp.float32)
+    chunks = model_width // 128
+    pairs = returned.reshape(slot_count, 2 * chunks, 128)[slot_of_pair]
+    out_pairs = pairs[:, :chunks]
+    grad_pairs = pairs[:, chunks:]
+    weighted = probs_flat[:, None, None] * out_pairs.astype(jnp.float32)
     mixed = jnp.sum(weighted.reshape(tok_rows, top_count, model_width), axis=1).astype(jnp.bfloat16)
     token_grad = jnp.sum(
         grad_pairs.astype(jnp.float32).reshape(tok_rows, top_count, model_width), axis=1

time: 406 us -> 402 us (level)
  local copies, waits for them, and re-layouts: 34.3 us -> 28.1 us
where the time goes in v8:
time: 402 us; the launch traced here: 401 us
  Pallas kernels  340 us (85%)
  local copies, waits for them, and re-layouts  28.1 us (7%)
  other arithmetic  17.2 us (4%)
  matrix products  15 us (4%)
    pallas_call x2, Pallas kernels, exchange(): pl.pallas_call(functools.partial(exchange_kernel, n_dp, n_ex, n_lo, bcast...  340 us

profile of v8, /device:TPU:75, one launch (start us, length us, event | category | flops | bytes accessed | tf_op | source)
XLA Modules:
  0.0 401.2 jit_solution(990148152080254544)
XLA Ops:
  0.6 0.0 copy-start
  0.6 0.8 copy.15
  1.5 0.1 reshape.174
  1.6 0.1 eq.39
  1.8 0.6 reduce-window.6
  2.4 0.2 slice_reduce_fusion
  2.6 0.1 fusion.24
  2.7 0.2 select_reduce_fusion
  2.9 0.0 copy-done
  2.9 0.0 copy-start.7
  2.9 2.4 gather_fusion.2
  5.4 0.0 copy-start.1
  5.4 0.1 fusion.21
  5.6 0.0 copy-done.7
  5.6 0.1 copy.14
  5.7 0.1 mul.72
  5.8 2.5 gather_fusion.1
  8.3 1.3 multiply_convert_fusion.1
  9.6 0.0 copy-done.1
  9.6 2.4 gather_fusion
  12.0 0.0 copy-start.2
  12.0 0.1 broadcast_select_fusion
  12.2 1.1 copy-done.2
  13.3 0.2 pad_maximum_fusion
  13.5 0.0 copy-start.4
  13.5 0.0 copy-start.5
  13.5 2.5 reshape.176.ex_send
  16.0 0.0 copy-done.4
  16.0 0.0 copy-done.5
  16.0 0.8 pad_maximum_fusion.2.dp_send
  16.9 159.6 %shard_map.85 = (bf16[32,288,128]{2,1,0:T(8,128)(2,1)}, bf16[16,128,2304]{2,1,0:T(8,128)(2,1)}) custom-call(bf16[32,288,128]{2,1,0:T(8,128)(2,1)} %reshape.176.ex_send, bf16[128,2304]{1,0:T(8,128)(2,1)} %pad_maximum_fusion.2.dp_send), custom_call_target="tpu_custom_call" | custom-call | tf_op jit(solution)/shard_map/pallas_call | solution.py:163
  176.5 3.7 reshape.177
  180.2 0.0 copy-start.3
  180.2 0.0 copy-start.8
  180.2 5.7 %fusion.2 = f32[288,1536]{1,0:T(8,128)S(1)} fusion(bf16[2048,2304]{1,0:T(8,128)(2,1)} %bitcast.36, bf16[288,4096]{1,0:T(8,128)(2,1)S(1)} %reshape.177), kind=kOutput, calls=%fused_computation.7 | convolution fusion | flops 1811939328 | bytes 9240576 | tf_op jit(solution)/shard_map/dot_general | solution.py:181
  185.9 0.0 copy-done.3
  185.9 0.6 copy-done.8
  186.5 1.4 multiply_convert_fusion.3
  187.9 2.0 fusion.8
  189.9 1.1 fusion.11
  191.0 0.2 pad_maximum_fusion.1
  191.3 2.5 reshape.179.ex_send
  193.8 4.8 %multiply_convert_fusion = bf16[2048,768]{1,0:T(8,128)(2,1)} fusion(bf16[288,768]{1,0:T(8,128)(2,1)S(1)} %get-tuple-element.15, bf16[288,4096]{1,0:T(8,128)(2,1)} %copy-done.3), kind=kOutput, calls=%fused_computation.4 | convolution fusion | flops 909115392 | bytes 4767744 | tf_op jit(solution)/shard_map/dot_general | solution.py:192
  198.7 0.0 copy-start.6
  198.7 180.3 %shard_map.86 = (bf16[32,288,128]{2,1,0:T(8,128)(2,1)}, bf16[16,128,768]{2,1,0:T(8,128)(2,1)}) custom-call(bf16[32,288,128]{2,1,0:T(8,128)(2,1)} %reshape.179.ex_send, bf16[16,128,768]{2,1,0:T(8,128)(2,1)} %bitcast.29), custom_call_target="tpu_custom_call" | custom-call | tf_op jit(solution)/shard_map/pallas_call | solution.py:163
  379.0 0.0 copy-done.6
  379.0 0.1 copy.18
  379.1 0.1 mul.90
  379.3 2.7 gather_fusion.3
  382.0 1.7 convert_multiply_fusion
  383.7 3.3 reshape.182
  387.0 5.0 %reduce_sum.56 = bf16[128,2048]{1,0:T(8,128)(2,1)} reduce(f32[128,2,2048]{2,1,0:T(2,128)} %reshape.182, f32[]{:T(128)} %constant.36.clone.1), dimensions={1}, to_apply=%region_5.6 | reduce | flops 262144 | bytes 2621444 | tf_op jit(solution)/shard_map/reduce_sum | solution.py:263
  392.0 1.2 slice.56
  393.1 1.3 reshape.183
  394.5 3.6 reduce.1
  398.1 3.0 reduce_sum.58
  (10 shorter events, 0.1 us)
Async XLA Ops:
  0.6 2.3 copy-start
  2.9 2.6 copy-start.7
  5.4 4.2 %copy-start.1 = (bf16[128,2048]{1,0:T(8,128)(2,1)S(1)}, bf16[128,2048]{1,0:T(8,128)(2,1)}, u32[]{:S(2)}) copy-start(bf16[128,2048]{1,0:T(8,128)(2,1)} %param.6) | copy-start | bytes 1572868
  12.0 1.3 copy-start.2
  13.5 2.5 copy-start.4
  13.5 2.5 copy-start.5
  180.2 5.7 %copy-start.3 = (bf16[288,4096]{1,0:T(8,128)(2,1)}, bf16[288,4096]{1,0:T(8,128)(2,1)S(1)}, u32[]{:S(2)}) copy-start(bf16[288,4096]{1,0:T(8,128)(2,1)S(1)} %reshape.177) | copy-start | bytes 7077892
  180.2 6.3 %copy-start.8 = (bf16[16,128,2304]{2,1,0:T(8,128)(2,1)S(1)}, bf16[16,128,2304]{2,1,0:T(8,128)(2,1)}, u32[]{:S(2)}) copy-start(bf16[16,128,2304]{2,1,0:T(8,128)(2,1)} %get-tuple-element.8) | copy-start | bytes 28311556
  198.7 180.3 %copy-start.6 = (s32[128,2]{0,1:T(2,128)S(1)}, s32[128,2]{0,1:T(2,128)}, u32[]{:S(2)}) copy-start(s32[128,2]{0,1:T(2,128)} %param.8) | copy-start | bytes 3076

commit v9 on v8

--- a/solution.py
+++ b/solution.py
@@ -79,7 +79,29 @@
     own_ex = pltpu.make_async_copy(ex_send.at[p], ex_recv.at[p], own_sems.at[0])
     own_ex.start()
     late = bcast and n_hi == 4
-    if not late:
+    n_x = n_ex // 8
+
+    def near_j(m):
+        a = m // 2
+        return lax.rem(p // 8 + a, n_x) * 8 + lax.rem(p // 2, 4) * 2 + lax.rem(p + m, 2)
+
+    def far_j(m):
+        b = 1 + m // (2 * n_x)
+        a = (m // 2) % n_x
+        return lax.rem(p // 8 + a, n_x) * 8 + lax.rem(p // 2 + b, 4) * 2 + lax.rem(p + m, 2)
+
+    def send_near(m, c):
+        ex_copy(near_j(m), p).start()
+        return c
+
+    def send_far(m, c):
+        ex_copy(far_j(m), p).start()
+        return c
+
+    split = late and far
+    if split:
+        lax.fori_loop(1, 2 * n_x, send_near, 0)
+    elif not late:
         lax.fori_loop(1, n_ex, send_ex, 0)
 
     def wait_ex(k, c):
@@ -128,7 +150,10 @@
         to_dn = fwd_copy(row * n_lo, n_lo, dn, 1, row)
         to_up.start()
         to_dn.start()
-        lax.fori_loop(1, n_ex, send_ex, 0)
+        if split:
+            lax.fori_loop(0, 6 * n_x, send_far, 0)
+        else:
+            lax.fori_loop(1, n_ex, send_ex, 0)
         fwd_copy(dn * n_lo, n_lo, dn, 0, dn).wait_recv()
         fwd_copy(up * n_lo, n_lo, up, 1, up).wait_recv()
         pass_up = fwd_copy(dn * n_lo, half, up, 2, 4)

time: 402 us -> 393 us (0.978)
  the two profiles are of different devices: /device:TPU:75 before, /device:TPU:87 now
where the time goes in v9:
time: 393 us; the launch traced here: 392 us
  Pallas kernels  331 us (84%)
  local copies, waits for them, and re-layouts  28.1 us (7%)
  other arithmetic  17.2 us (4%)
  matrix products  15 us (4%)
    pallas_call x2, Pallas kernels, exchange(): pl.pallas_call(functools.partial(exchange_kernel, n_dp, n_ex, n_lo, bcast...  331 us

profile of v9, /device:TPU:87, one launch (start us, length us, event | category | flops | bytes accessed | tf_op | source)
XLA Modules:
  0.0 392.2 jit_solution(1479225298126652904)
XLA Ops:
  0.6 0.0 copy-start
  0.6 0.8 copy.15
  1.5 0.1 reshape.174
  1.6 0.1 eq.39
  1.8 0.6 reduce-window.6
  2.4 0.2 slice_reduce_fusion
  2.6 0.1 fusion.24
  2.7 0.2 select_reduce_fusion
  2.9 0.0 copy-done
  2.9 0.0 copy-start.7
  2.9 2.4 gather_fusion.2
  5.4 0.0 copy-start.1
  5.4 0.1 fusion.21
  5.6 0.0 copy-done.7
  5.6 0.1 copy.14
  5.7 0.1 mul.72
  5.8 2.5 gather_fusion.1
  8.3 1.3 multiply_convert_fusion.1
  9.6 0.0 copy-done.1
  9.6 2.4 gather_fusion
  12.0 0.0 copy-start.2
  12.0 0.1 broadcast_select_fusion
  12.2 1.1 copy-done.2
  13.3 0.2 pad_maximum_fusion
  13.5 0.0 copy-start.4
  13.5 0.0 copy-start.5
  13.5 2.5 reshape.176.ex_send
  16.0 0.0 copy-done.4
  16.0 0.0 copy-done.5
  16.0 0.8 pad_maximum_fusion.2.dp_send
  16.9 155.3 %shard_map.85 = (bf16[32,288,128]{2,1,0:T(8,128)(2,1)}, bf16[16,128,2304]{2,1,0:T(8,128)(2,1)}) custom-call(bf16[32,288,128]{2,1,0:T(8,128)(2,1)} %reshape.176.ex_send, bf16[128,2304]{1,0:T(8,128)(2,1)} %pad_maximum_fusion.2.dp_send), custom_call_target="tpu_custom_call" | custom-call | tf_op jit(solution)/shard_map/pallas_call | solution.py:188
  172.2 3.7 reshape.177
  175.9 0.0 copy-start.3
  175.9 0.0 copy-start.8
  175.9 5.7 %fusion.2 = f32[288,1536]{1,0:T(8,128)S(1)} fusion(bf16[2048,2304]{1,0:T(8,128)(2,1)} %bitcast.36, bf16[288,4096]{1,0:T(8,128)(2,1)S(1)} %reshape.177), kind=kOutput, calls=%fused_computation.7 | convolution fusion | flops 1811939328 | bytes 9240576 | tf_op jit(solution)/shard_map/dot_general | solution.py:206
  181.6 0.0 copy-done.3
  181.6 0.6 copy-done.8
  182.2 1.4 multiply_convert_fusion.3
  183.6 2.0 fusion.8
  185.6 1.1 fusion.11
  186.7 0.2 pad_maximum_fusion.1
  187.0 2.5 reshape.179.ex_send
  189.5 4.8 %multiply_convert_fusion = bf16[2048,768]{1,0:T(8,128)(2,1)} fusion(bf16[288,768]{1,0:T(8,128)(2,1)S(1)} %get-tuple-element.15, bf16[288,4096]{1,0:T(8,128)(2,1)} %copy-done.3), kind=kOutput, calls=%fused_computation.4 | convolution fusion | flops 909115392 | bytes 4767744 | tf_op jit(solution)/shard_map/dot_general | solution.py:217
  194.3 0.0 copy-start.6
  194.3 175.7 %shard_map.86 = (bf16[32,288,128]{2,1,0:T(8,128)(2,1)}, bf16[16,128,768]{2,1,0:T(8,128)(2,1)}) custom-call(bf16[32,288,128]{2,1,0:T(8,128)(2,1)} %reshape.179.ex_send, bf16[16,128,768]{2,1,0:T(8,128)(2,1)} %bitcast.29), custom_call_target="tpu_custom_call" | custom-call | tf_op jit(solution)/shard_map/pallas_call | solution.py:188
  370.0 0.0 copy-done.6
  370.1 0.1 copy.18
  370.2 0.1 mul.90
  370.3 2.7 gather_fusion.3
  373.0 1.7 convert_multiply_fusion
  374.7 3.3 reshape.182
  378.0 5.0 %reduce_sum.56 = bf16[128,2048]{1,0:T(8,128)(2,1)} reduce(f32[128,2,2048]{2,1,0:T(2,128)} %reshape.182, f32[]{:T(128)} %constant.36.clone.1), dimensions={1}, to_apply=%region_5.6 | reduce | flops 262144 | bytes 2621444 | tf_op jit(solution)/shard_map/reduce_sum | solution.py:288
  383.0 1.2 slice.56
  384.2 1.3 reshape.183
  385.5 3.6 reduce.1
  389.2 3.0 reduce_sum.58
  (10 shorter events, 0.1 us)
Async XLA Ops:
  0.6 2.3 copy-start
  2.9 2.6 copy-start.7
  5.4 4.2 %copy-start.1 = (bf16[128,2048]{1,0:T(8,128)(2,1)S(1)}, bf16[128,2048]{1,0:T(8,128)(2,1)}, u32[]{:S(2)}) copy-start(bf16[128,2048]{1,0:T(8,128)(2,1)} %param.6) | copy-start | bytes 1572868
  12.0 1.3 copy-start.2
  13.5 2.5 copy-start.4
  13.5 2.5 copy-start.5
  175.9 5.7 %copy-start.3 = (bf16[288,4096]{1,0:T(8,128)(2,1)}, bf16[288,4096]{1,0:T(8,128)(2,1)S(1)}, u32[]{:S(2)}) copy-start(bf16[288,4096]{1,0:T(8,128)(2,1)S(1)} %reshape.177) | copy-start | bytes 7077892
  175.9 6.3 %copy-start.8 = (bf16[16,128,2304]{2,1,0:T(8,128)(2,1)S(1)}, bf16[16,128,2304]{2,1,0:T(8,128)(2,1)}, u32[]{:S(2)}) copy-start(bf16[16,128,2304]{2,1,0:T(8,128)(2,1)} %get-tuple-element.8) | copy-start | bytes 28311556
  194.3 175.7 %copy-start.6 = (s32[128,2]{0,1:T(2,128)S(1)}, s32[128,2]{0,1:T(2,128)}, u32[]{:S(2)}) copy-start(s32[128,2]{0,1:T(2,128)} %param.8) | copy-start | bytes 3076

commit v10 on v9

--- a/solution.py
+++ b/solution.py
@@ -71,7 +71,24 @@
         return c
 
     own_dp = pltpu.make_async_copy(dp_send if bcast else dp_send.at[q], dp_recv.at[q], own_sems.at[1])
-    if bcast:
+    chain = bcast and n_hi == 4 and n_lo == 4
+
+    def lo_copy(origin, target, s_idx, own):
+        slot = row * n_lo + origin
+        return pltpu.make_async_remote_copy(
+            src_ref=dp_send if own else dp_recv.at[slot], dst_ref=dp_recv.at[slot],
+            send_sem=send_sems.at[n_ex + s_idx], recv_sem=recv_sems.at[n_ex + slot],
+            device_id=(row * n_lo + target, p), device_id_type=MESH)
+
+    if chain:
+        @pl.when(lo < n_lo - 1)
+        def _():
+            lo_copy(lo, lo + 1, 0, True).start()
+
+        @pl.when(lo > 0)
+        def _():
+            lo_copy(lo, lo - 1, 4, True).start()
+    elif bcast:
         lax.fori_loop(1, n_lo, send_lo, 0)
     else:
         lax.fori_loop(1, n_dp, send_dp, 0)
@@ -144,7 +161,42 @@
         up = lax.rem(row + 1, 4)
         dn = lax.rem(row + 3, 4)
         far_row = lax.rem(row + 2, 4)
-        lax.fori_loop(1, n_lo, wait_lo, 0)
+        if chain:
+            for step in range(1, n_lo):
+                @pl.when(lo - step >= 0)
+                def _():
+                    lo_copy(lo - step, lo, step, False).wait_recv()
+
+                    @pl.when(lo < n_lo - 1)
+                    def _():
+                        lo_copy(lo - step, lo + 1, step, False).start()
+
+                @pl.when(lo + step <= n_lo - 1)
+                def _():
+                    lo_copy(lo + step, lo, 4 + step, False).wait_recv()
+
+                    @pl.when(lo > 0)
+                    def _():
+                        lo_copy(lo + step, lo - 1, 4 + step, False).start()
+
+            @pl.when(lo < n_lo - 1)
+            def _():
+                lo_copy(lo, lo + 1, 0, True).wait_send()
+
+            @pl.when(lo > 0)
+            def _():
+                lo_copy(lo, lo - 1, 4, True).wait_send()
+
+            for step in range(1, n_lo):
+                @pl.when((lo - step >= 0) & (lo < n_lo - 1))
+                def _():
+                    lo_copy(lo - step, lo + 1, step, False).wait_send()
+
+                @pl.when((lo + step <= n_lo - 1) & (lo > 0))
+                def _():
+                    lo_copy(lo + step, lo - 1, 4 + step, False).wait_send()
+        else:
+            lax.fori_loop(1, n_lo, wait_lo, 0)
         own_dp.wait()
         to_up = fwd_copy(row * n_lo, n_lo, up, 0, row)
         to_dn = fwd_copy(row * n_lo, n_lo, dn, 1, row)

time: 393 us -> 390 us (level)
  the two profiles are of different devices: /device:TPU:87 before, /device:TPU:111 now
where the time goes in v10:
time: 390 us; the launch traced here: 389 us
  Pallas kernels  328 us (84%)
  local copies, waits for them, and re-layouts  28.1 us (7%)
  other arithmetic  17.2 us (4%)
  matrix products  15 us (4%)
    pallas_call x2, Pallas kernels, exchange(): pl.pallas_call(functools.partial(exchange_kernel, n_dp, n_ex, n_lo, bcast...  328 us

profile of v10, /device:TPU:111, one launch (start us, length us, event | category | flops | bytes accessed | tf_op | source)
XLA Modules:
  0.0 389.3 jit_solution(5785916422802700756)
XLA Ops:
  0.6 0.0 copy-start
  0.6 0.8 copy.15
  1.5 0.1 reshape.174
  1.6 0.1 eq.39
  1.8 0.6 reduce-window.6
  2.4 0.2 slice_reduce_fusion
  2.6 0.1 fusion.24
  2.7 0.2 select_reduce_fusion
  2.9 0.0 copy-done
  2.9 0.0 copy-start.7
  2.9 2.4 gather_fusion.2
  5.4 0.0 copy-start.1
  5.4 0.1 fusion.21
  5.6 0.0 copy-done.7
  5.6 0.1 copy.14
  5.7 0.1 mul.72
  5.8 2.5 gather_fusion.1
  8.3 1.3 multiply_convert_fusion.1
  9.6 0.0 copy-done.1
  9.6 2.4 gather_fusion
  12.0 0.0 copy-start.2
  12.0 0.1 broadcast_select_fusion
  12.2 1.1 copy-done.2
  13.3 0.2 pad_maximum_fusion
  13.5 0.0 copy-start.4
  13.5 0.0 copy-start.5
  13.5 2.5 reshape.176.ex_send
  16.0 0.0 copy-done.4
  16.0 0.0 copy-done.5
  16.0 0.8 pad_maximum_fusion.2.dp_send
  16.9 148.9 %shard_map.85 = (bf16[32,288,128]{2,1,0:T(8,128)(2,1)}, bf16[16,128,2304]{2,1,0:T(8,128)(2,1)}) custom-call(bf16[32,288,128]{2,1,0:T(8,128)(2,1)} %reshape.176.ex_send, bf16[128,2304]{1,0:T(8,128)(2,1)} %pad_maximum_fusion.2.dp_send), custom_call_target="tpu_custom_call" | custom-call | tf_op jit(solution)/shard_map/pallas_call | solution.py:240
  165.8 3.7 reshape.177
  169.4 0.0 copy-start.3
  169.4 0.0 copy-start.8
  169.4 5.7 %fusion.2 = f32[288,1536]{1,0:T(8,128)S(1)} fusion(bf16[2048,2304]{1,0:T(8,128)(2,1)} %bitcast.36, bf16[288,4096]{1,0:T(8,128)(2,1)S(1)} %reshape.177), kind=kOutput, calls=%fused_computation.7 | convolution fusion | flops 1811939328 | bytes 9240576 | tf_op jit(solution)/shard_map/dot_general | solution.py:258
  175.1 0.0 copy-done.3
  175.1 0.6 copy-done.8
  175.8 1.4 multiply_convert_fusion.3
  177.2 2.0 fusion.8
  179.2 1.1 fusion.11
  180.3 0.2 pad_maximum_fusion.1
  180.6 2.5 reshape.179.ex_send
  183.1 4.8 %multiply_convert_fusion = bf16[2048,768]{1,0:T(8,128)(2,1)} fusion(bf16[288,768]{1,0:T(8,128)(2,1)S(1)} %get-tuple-element.15, bf16[288,4096]{1,0:T(8,128)(2,1)} %copy-done.3), kind=kOutput, calls=%fused_computation.4 | convolution fusion | flops 909115392 | bytes 4767744 | tf_op jit(solution)/shard_map/dot_general | solution.py:269
  187.9 0.0 copy-start.6
  187.9 179.2 %shard_map.86 = (bf16[32,288,128]{2,1,0:T(8,128)(2,1)}, bf16[16,128,768]{2,1,0:T(8,128)(2,1)}) custom-call(bf16[32,288,128]{2,1,0:T(8,128)(2,1)} %reshape.179.ex_send, bf16[16,128,768]{2,1,0:T(8,128)(2,1)} %bitcast.29), custom_call_target="tpu_custom_call" | custom-call | tf_op jit(solution)/shard_map/pallas_call | solution.py:240
  367.1 0.0 copy-done.6
  367.1 0.1 copy.18
  367.2 0.1 mul.90
  367.4 2.7 gather_fusion.3
  370.1 1.7 convert_multiply_fusion
  371.8 3.3 reshape.182
  375.1 5.0 %reduce_sum.56 = bf16[128,2048]{1,0:T(8,128)(2,1)} reduce(f32[128,2,2048]{2,1,0:T(2,128)} %reshape.182, f32[]{:T(128)} %constant.36.clone.1), dimensions={1}, to_apply=%region_5.6 | reduce | flops 262144 | bytes 2621444 | tf_op jit(solution)/shard_map/reduce_sum | solution.py:340
  380.1 1.2 slice.56
  381.3 1.3 reshape.183
  382.6 3.6 reduce.1
  386.2 3.0 reduce_sum.58
  (10 shorter events, 0.1 us)
Async XLA Ops:
  0.6 2.3 copy-start
  2.9 2.6 copy-start.7
  5.4 4.2 %copy-start.1 = (bf16[128,2048]{1,0:T(8,128)(2,1)S(1)}, bf16[128,2048]{1,0:T(8,128)(2,1)}, u32[]{:S(2)}) copy-start(bf16[128,2048]{1,0:T(8,128)(2,1)} %param.6) | copy-start | bytes 1572868
  12.0 1.3 copy-start.2
  13.5 2.5 copy-start.4
  13.5 2.5 copy-start.5
  169.4 5.7 %copy-start.3 = (bf16[288,4096]{1,0:T(8,128)(2,1)}, bf16[288,4096]{1,0:T(8,128)(2,1)S(1)}, u32[]{:S(2)}) copy-start(bf16[288,4096]{1,0:T(8,128)(2,1)S(1)} %reshape.177) | copy-start | bytes 7077892
  169.4 6.3 %copy-start.8 = (bf16[16,128,2304]{2,1,0:T(8,128)(2,1)S(1)}, bf16[16,128,2304]{2,1,0:T(8,128)(2,1)}, u32[]{:S(2)}) copy-start(bf16[16,128,2304]{2,1,0:T(8,128)(2,1)} %get-tuple-element.8) | copy-start | bytes 28311556
  187.9 179.2 %copy-start.6 = (s32[128,2]{0,1:T(2,128)S(1)}, s32[128,2]{0,1:T(2,128)}, u32[]{:S(2)}) copy-start(s32[128,2]{0,1:T(2,128)} %param.8) | copy-start | bytes 3076

commit v11 on v10

--- a/solution.py
+++ b/solution.py
@@ -297,10 +297,15 @@
     token_of_slot = source // top_count
     probs_flat = gate_probs.reshape(pair_count)
     weight_slot = jnp.where(filled, probs_flat[source], jnp.float32(0.0))
-    send_rows = jnp.where(filled[:, None], tokens[token_of_slot], jnp.zeros((), jnp.bfloat16))
-    send_grad = (weight_slot[:, None] * out_grad[token_of_slot].astype(jnp.float32)).astype(
-        jnp.bfloat16
-    )
+    chunks = model_width // 128
+    tok_chunks = tokens.reshape(tok_rows, chunks, 128)
+    grad_chunks = out_grad.reshape(tok_rows, chunks, 128)
+    send_rows = jnp.where(
+        filled[:, None, None], tok_chunks[token_of_slot], jnp.zeros((), jnp.bfloat16)
+    )
+    send_grad = (
+        weight_slot[:, None, None] * grad_chunks[token_of_slot].astype(jnp.float32)
+    ).astype(jnp.bfloat16)
     block_shape = (peer_count, local_count * capacity * 2 * model_width // 128, 128)
     send_both = jnp.concatenate([send_rows, send_grad], axis=1).reshape(block_shape)
     gate_width = gate_up_weight.shape[2]
@@ -329,10 +334,13 @@
         pre_grad, full_gate_up, (((1,), (1,)), ((), ())), preferred_element_type=jnp.float32
     )
     back_both = jnp.concatenate(
-        [produced.astype(jnp.bfloat16), input_grad.astype(jnp.bfloat16)], axis=1
+        [
+            produced.astype(jnp.bfloat16).reshape(slot_count, chunks, 128),
+            input_grad.astype(jnp.bfloat16).reshape(slot_count, chunks, 128),
+        ],
+        axis=1,
     ).reshape(block_shape)
     returned, down_recv = exchange(back_both, down_parts, False, 1)
-    chunks = model_width // 128
     pairs = returned.reshape(slot_count, 2 * chunks, 128)[slot_of_pair]
     out_pairs = pairs[:, :chunks]
     grad_pairs = pairs[:, chunks:]

time: 390 us -> 383 us (0.982)
  local copies, waits for them, and re-layouts: 28.1 us -> 20.3 us
    reshape x2 -> x0, local copies, waits for them, and re-layouts: 5 us -> none  [the longest x1 2.54 us: shards(): back_both = jnp.concatenate([produced.astype(jnp.bfloat16), input_grad.as...]
where the time goes in v11:
time: 383 us
  Pallas kernels  328 us (86%)
  local copies, waits for them, and re-layouts  20.3 us (5%)
  other arithmetic  20.3 us (5%)
  matrix products  13 us (3%)
    pallas_call x2, Pallas kernels, exchange(): pl.pallas_call(functools.partial(exchange_kernel, n_dp, n_ex, n_lo, bcast...  328 us

profile of v11, /device:TPU:111, one launch (start us, length us, event | category | flops | bytes accessed | tf_op | source)
XLA Modules:
  0.0 382.5 jit_solution(3352065851098730810)
XLA Ops:
  0.6 0.0 copy-start.4
  0.6 1.1 copy.21
  1.8 0.8 copy.15
  2.6 0.1 reshape.186
  2.7 0.1 eq.39
  2.9 0.6 reduce-window.6
  3.5 0.2 slice_reduce_fusion
  3.7 0.1 fusion.30
  3.8 0.2 select_reduce_fusion
  4.0 1.8 gather_fusion.2
  5.9 0.0 copy-start
  5.9 0.1 fusion.27
  6.0 0.0 copy-done.4
  6.0 0.1 copy.14
  6.1 0.1 mul.72
  6.3 2.5 gather_fusion.1
  8.8 0.4 multiply_convert_fusion.1
  9.1 0.0 copy-done
  9.1 0.1 copy.20
  9.3 1.8 gather_fusion
  11.1 1.0 broadcast_select_fusion
  12.1 0.0 copy-start.1
  12.1 0.0 copy-start.2
  12.2 1.8 pad_maximum_fusion
  14.0 0.0 copy-done.1
  14.0 0.0 copy-done.2
  14.0 0.8 pad_maximum_fusion.2.dp_send
  14.8 148.9 %shard_map.85 = (bf16[32,288,128]{2,1,0:T(8,128)(2,1)}, bf16[16,128,2304]{2,1,0:T(8,128)(2,1)}) custom-call(bf16[32,288,128]{2,1,0:T(8,128)(2,1)} %bitcast.41, bf16[128,2304]{1,0:T(8,128)(2,1)} %pad_maximum_fusion.2.dp_send), custom_call_target="tpu_custom_call" | custom-call | tf_op jit(solution)/shard_map/pallas_call | solution.py:240
  163.7 3.7 reshape.191
  167.4 0.0 copy-start.5
  167.4 4.9 %fusion.2 = f32[288,1536]{1,0:T(8,128)S(1)} fusion(bf16[2048,2304]{1,0:T(8,128)(2,1)} %bitcast.56, bf16[288,4096]{1,0:T(8,128)(2,1)S(1)} %reshape.191), kind=kOutput, calls=%fused_computation.7 | convolution fusion | flops 1811939328 | bytes 9240576 | tf_op jit(solution)/shard_map/dot_general | solution.py:258
  172.3 0.5 copy-done.5
  172.9 1.4 multiply_convert_fusion.3
  174.3 2.1 fusion.14
  176.3 0.2 copy.23
  176.6 1.1 fusion.17
  177.7 0.2 copy.22
  178.0 1.8 pad_maximum_fusion.1
  179.8 3.5 multiply_convert_fusion
  183.3 0.0 copy-start.3
  183.3 179.1 %shard_map.86 = (bf16[32,288,128]{2,1,0:T(8,128)(2,1)}, bf16[16,128,768]{2,1,0:T(8,128)(2,1)}) custom-call(bf16[32,288,128]{2,1,0:T(8,128)(2,1)} %bitcast.42, bf16[16,128,768]{2,1,0:T(8,128)(2,1)} %bitcast.47), custom_call_target="tpu_custom_call" | custom-call | tf_op jit(solution)/shard_map/pallas_call | solution.py:240
  362.4 0.0 copy-done.3
  362.4 0.1 copy.18
  362.5 0.1 mul.90
  362.7 2.7 gather_fusion.3
  365.4 1.7 convert_multiply_fusion
  367.1 3.3 reshape.198
  370.4 5.0 %reduce_sum.56 = bf16[128,2048]{1,0:T(8,128)(2,1)} reduce(f32[128,2,2048]{2,1,0:T(2,128)} %reshape.198, f32[]{:T(128)} %constant.36.clone.1), dimensions={1}, to_apply=%region_5.6 | reduce | flops 262144 | bytes 2621444 | tf_op jit(solution)/shard_map/reduce_sum | solution.py:348
  375.4 0.2 slice.56
  375.5 0.3 reshape.199
  375.8 3.6 reduce.1
  379.5 3.0 reduce_sum.58
  (10 shorter events, 0.1 us)
Async XLA Ops:
  0.6 5.4 %copy-start.4 = (f32[128,2]{0,1:T(2,128)S(1)}, f32[128,2]{0,1:T(2,128)}, u32[]{:S(2)}) copy-start(f32[128,2]{0,1:T(2,128)} %param.9) | copy-start | bytes 3076
  5.9 3.3 copy-start
  12.1 1.8 copy-start.1
  12.1 1.8 copy-start.2
  167.4 5.5 %copy-start.5 = (bf16[16,128,2304]{2,1,0:T(8,128)(2,1)S(1)}, bf16[16,128,2304]{2,1,0:T(8,128)(2,1)}, u32[]{:S(2)}) copy-start(bf16[16,128,2304]{2,1,0:T(8,128)(2,1)} %get-tuple-element.8) | copy-start | bytes 28311556
  183.3 179.1 %copy-start.3 = (s32[128,2]{0,1:T(2,128)S(1)}, s32[128,2]{0,1:T(2,128)}, u32[]{:S(2)}) copy-start(s32[128,2]{0,1:T(2,128)} %param.8) | copy-start | bytes 3076

commit v12 on v11

--- a/solution.py
+++ b/solution.py
@@ -255,7 +255,12 @@
 
 
 def swiglu_forward(expert_rows, gate_up_full):
-    projected = jnp.dot(expert_rows, gate_up_full, preferred_element_type=jnp.float32)
+    projected = lax.dot_general(
+        expert_rows,
+        gate_up_full.reshape(expert_rows.shape[1], expert_rows.shape[2], -1),
+        (((1, 2), (0, 1)), ((), ())),
+        preferred_element_type=jnp.float32,
+    )
     units = gate_up_full.shape[1] // 2
     gate_part = projected[:, :units]
     up_part = projected[:, units:]
@@ -270,7 +275,7 @@
         grad_rows, hidden, (((0,), (0,)), ((), ())), preferred_element_type=jnp.float32
     )
     parts = lax.axis_size("dp")
-    blocks = (product * loss_scale).astype(jnp.bfloat16)
+    blocks = (product * loss_scale).astype(jnp.bfloat16).reshape(-1, hidden.shape[1])
     return blocks.reshape(parts, blocks.shape[0] // parts, blocks.shape[1])
 
 
@@ -311,9 +316,9 @@
     gate_width = gate_up_weight.shape[2]
     joined = jnp.concatenate([gate_up_weight[0], down_weight[0]], axis=1)
     recv_both, gathered = exchange(send_both, joined, True, 0)
-    recv_both = recv_both.reshape(-1, 2 * model_width)
-    expert_rows = recv_both[:, :model_width]
-    grad_rows = recv_both[:, model_width:]
+    recv_both = recv_both.reshape(slot_count, 2 * chunks, 128)
+    expert_rows = recv_both[:, :chunks]
+    grad_rows = recv_both[:, chunks:]
     full_joined = gathered.reshape(-1, joined.shape[1])
     full_gate_up = full_joined[:, :gate_width]
     full_down = full_joined[:, gate_width:]
@@ -322,7 +327,12 @@
         hidden, full_down, (((1,), (1,)), ((), ())), preferred_element_type=jnp.float32
     )
     down_parts = weight_blocks(grad_rows, hidden)
-    hidden_grad = jnp.dot(grad_rows, full_down, preferred_element_type=jnp.float32)
+    hidden_grad = lax.dot_general(
+        grad_rows,
+        full_down.reshape(chunks, 128, -1),
+        (((1, 2), (0, 1)), ((), ())),
+        preferred_element_type=jnp.float32,
+    )
     pre_grad = jnp.concatenate(
         [
             hidden_grad * up_part * sigmoid_gate * (1.0 + gate_part * (1.0 - sigmoid_gate)),

time: 383 us -> 381 us (level)
    slice x1 -> x4, local copies, waits for them, and re-layouts: 0.18 us -> 4.13 us  [the longest x1 3.34 us: shards(): full_gate_up = full_joined[:, :gate_width]]
where the time goes in v12:
time: 381 us
  Pallas kernels  328 us (86%)
  local copies, waits for them, and re-layouts  21.2 us (6%)
  other arithmetic  20.4 us (5%)
  matrix products  10.1 us (3%)
    pallas_call x2, Pallas kernels, exchange(): pl.pallas_call(functools.partial(exchange_kernel, n_dp, n_ex, n_lo, bcast...  328 us

profile of v12, /device:TPU:111, one launch (start us, length us, event | category | flops | bytes accessed | tf_op | source)
XLA Modules:
  0.0 380.7 jit_solution(11873643144693878582)
XLA Ops:
  0.6 0.0 copy-start.1
  0.6 0.8 copy.19
  1.5 0.1 eq.39
  1.6 0.6 reduce-window.6
  2.2 0.2 slice_reduce_fusion
  2.5 0.1 reshape.189
  2.6 0.1 fusion.13
  2.7 0.2 select_reduce_fusion
  2.9 0.8 copy.18
  3.7 0.1 mul.72
  3.8 2.5 gather_fusion.1
  6.3 0.1 fusion.10
  6.5 0.0 copy-done.1
  6.5 0.1 copy.29
  6.6 0.0 copy-start.2
  6.6 1.8 gather_fusion.2
  8.5 0.4 multiply_convert_fusion.1
  8.8 0.0 copy-done.2
  8.8 0.1 copy.28
  9.0 1.8 gather_fusion
  10.8 1.0 broadcast_select_fusion
  11.8 0.0 copy-start.3
  11.9 0.0 copy-start.4
  11.9 1.8 pad_maximum_fusion
  13.7 0.0 copy-done.3
  13.7 0.0 copy-done.4
  13.7 0.8 pad_maximum_fusion.2.dp_send
  14.5 149.1 %shard_map.85 = (bf16[32,288,128]{2,1,0:T(8,128)(2,1)}, bf16[16,128,2304]{2,1,0:T(8,128)(2,1)}) custom-call(bf16[32,288,128]{2,1,0:T(8,128)(2,1)} %bitcast.57, bf16[128,2304]{1,0:T(8,128)(2,1)} %pad_maximum_fusion.2.dp_send), custom_call_target="tpu_custom_call" | custom-call | tf_op jit(solution)/shard_map/pallas_call | solution.py:240
  163.6 0.0 copy-start
  163.6 3.3 slice.50
  167.0 0.1 copy-done
  167.1 0.0 slice-start
  167.1 0.4 fusion.20
  167.5 0.0 slice-start.1
  167.5 0.0 slice-start.2
  167.5 2.0 convolution_bitcast_fusion
  169.5 0.0 slice-done
  169.5 1.1 slice-done.1
  170.6 0.2 slice-done.2
  170.9 0.2 slice.53
  171.1 1.3 multiply_convert_fusion.3
  172.4 3.6 multiply_convert_fusion.dp_send
  176.0 1.1 fusion
  177.1 0.2 copy.30
  177.4 2.0 fusion.1
  179.4 0.2 copy.31
  179.6 1.8 pad_maximum_fusion.1
  181.5 0.0 copy-start.5
  181.5 179.0 %shard_map.86 = (bf16[32,288,128]{2,1,0:T(8,128)(2,1)}, bf16[16,128,768]{2,1,0:T(8,128)(2,1)}) custom-call(bf16[32,288,128]{2,1,0:T(8,128)(2,1)} %bitcast.58, bf16[16,128,768]{2,1,0:T(8,128)(2,1)} %multiply_convert_fusion.dp_send), custom_call_target="tpu_custom_call" | custom-call | tf_op jit(solution)/shard_map/pallas_call | solution.py:240
  360.5 0.0 copy-done.5
  360.5 0.1 copy.24
  360.7 0.1 mul.90
  360.8 2.7 gather_fusion.3
  363.5 1.7 convert_multiply_fusion
  365.2 3.3 reshape.202
  368.5 5.0 %reduce_sum.56 = bf16[128,2048]{1,0:T(8,128)(2,1)} reduce(f32[128,2,2048]{2,1,0:T(2,128)} %reshape.202, f32[]{:T(128)} %constant.36.clone.1), dimensions={1}, to_apply=%region_5.6 | reduce | flops 262144 | bytes 2621444 | tf_op jit(solution)/shard_map/reduce_sum | solution.py:358
  373.5 0.2 slice.56
  373.7 0.3 reshape.203
  374.0 3.7 reduce.1
  377.7 3.0 reduce_sum.58
  (11 shorter events, 0.1 us)
Async XLA Ops:
  0.6 5.8 %copy-start.1 = (bf16[128,2048]{1,0:T(8,128)(2,1)S(1)}, bf16[128,2048]{1,0:T(8,128)(2,1)}, u32[]{:S(2)}) copy-start(bf16[128,2048]{1,0:T(8,128)(2,1)} %param.7) | copy-start | bytes 1572868
  6.6 2.2 copy-start.2
  11.8 1.8 copy-start.3
  11.9 1.8 copy-start.4
  163.6 3.5 copy-start
  167.1 2.5 slice-start
  167.5 3.2 slice-start.1
  167.5 3.4 slice-start.2
  181.5 179.1 %copy-start.5 = (s32[128,2]{0,1:T(2,128)S(1)}, s32[128,2]{0,1:T(2,128)}, u32[]{:S(2)}) copy-start(s32[128,2]{0,1:T(2,128)} %param.8) | copy-start | bytes 3076

commit v13 on v12

--- a/solution.py
+++ b/solution.py
@@ -71,6 +71,7 @@
         return c
 
     own_dp = pltpu.make_async_copy(dp_send if bcast else dp_send.at[q], dp_recv.at[q], own_sems.at[1])
+    own_dp.start()
     chain = bcast and n_hi == 4 and n_lo == 4
 
     def lo_copy(origin, target, s_idx, own):
@@ -92,7 +93,6 @@
         lax.fori_loop(1, n_lo, send_lo, 0)
     else:
         lax.fori_loop(1, n_dp, send_dp, 0)
-    own_dp.start()
     own_ex = pltpu.make_async_copy(ex_send.at[p], ex_recv.at[p], own_sems.at[0])
     own_ex.start()
     late = bcast and n_hi == 4

time: 381 us -> 381 us (level)
  no operation moved by 1% of the time
where the time goes in v13:
time: 381 us
  Pallas kernels  328 us (86%)
  local copies, waits for them, and re-layouts  21.2 us (6%)
  other arithmetic  20.4 us (5%)
  matrix products  10.1 us (3%)
    pallas_call x2, Pallas kernels, exchange(): pl.pallas_call(functools.partial(exchange_kernel, n_dp, n_ex, n_lo, bcast...  328 us

profile of v13, /device:TPU:111, one launch (start us, length us, event | category | flops | bytes accessed | tf_op | source)
XLA Modules:
  0.0 381.0 jit_solution(13045236206009020708)
XLA Ops:
  0.6 0.0 copy-start.1
  0.6 0.8 copy.19
  1.5 0.1 eq.39
  1.6 0.6 reduce-window.6
  2.2 0.2 slice_reduce_fusion
  2.5 0.1 reshape.189
  2.6 0.1 fusion.13
  2.7 0.2 select_reduce_fusion
  2.9 0.8 copy.18
  3.7 0.1 mul.72
  3.8 2.5 gather_fusion.1
  6.3 0.1 fusion.10
  6.5 0.0 copy-done.1
  6.5 0.1 copy.29
  6.6 0.0 copy-start.2
  6.6 1.8 gather_fusion.2
  8.5 0.4 multiply_convert_fusion.1
  8.8 0.0 copy-done.2
  8.8 0.1 copy.28
  9.0 1.8 gather_fusion
  10.8 1.0 broadcast_select_fusion
  11.8 0.0 copy-start.3
  11.9 0.0 copy-start.4
  11.9 1.8 pad_maximum_fusion
  13.7 0.0 copy-done.3
  13.7 0.0 copy-done.4
  13.7 0.8 pad_maximum_fusion.2.dp_send
  14.5 149.1 %shard_map.85 = (bf16[32,288,128]{2,1,0:T(8,128)(2,1)}, bf16[16,128,2304]{2,1,0:T(8,128)(2,1)}) custom-call(bf16[32,288,128]{2,1,0:T(8,128)(2,1)} %bitcast.57, bf16[128,2304]{1,0:T(8,128)(2,1)} %pad_maximum_fusion.2.dp_send), custom_call_target="tpu_custom_call" | custom-call | tf_op jit(solution)/shard_map/pallas_call | solution.py:240
  163.6 0.0 copy-start
  163.6 3.3 slice.50
  167.0 0.1 copy-done
  167.1 0.0 slice-start
  167.1 0.4 fusion.20
  167.5 0.0 slice-start.1
  167.5 0.0 slice-start.2
  167.5 2.0 convolution_bitcast_fusion
  169.5 0.0 slice-done
  169.5 1.1 slice-done.1
  170.6 0.2 slice-done.2
  170.9 0.2 slice.53
  171.1 1.3 multiply_convert_fusion.3
  172.4 3.6 multiply_convert_fusion.dp_send
  176.0 1.1 fusion
  177.1 0.2 copy.30
  177.4 2.0 fusion.1
  179.4 0.2 copy.31
  179.6 1.8 pad_maximum_fusion.1
  181.5 0.0 copy-start.5
  181.5 179.3 %shard_map.86 = (bf16[32,288,128]{2,1,0:T(8,128)(2,1)}, bf16[16,128,768]{2,1,0:T(8,128)(2,1)}) custom-call(bf16[32,288,128]{2,1,0:T(8,128)(2,1)} %bitcast.58, bf16[16,128,768]{2,1,0:T(8,128)(2,1)} %multiply_convert_fusion.dp_send), custom_call_target="tpu_custom_call" | custom-call | tf_op jit(solution)/shard_map/pallas_call | solution.py:240
  360.7 0.0 copy-done.5
  360.8 0.1 copy.24
  360.9 0.1 mul.90
  361.0 2.7 gather_fusion.3
  363.7 1.7 convert_multiply_fusion
  365.4 3.3 reshape.202
  368.7 5.0 %reduce_sum.56 = bf16[128,2048]{1,0:T(8,128)(2,1)} reduce(f32[128,2,2048]{2,1,0:T(2,128)} %reshape.202, f32[]{:T(128)} %constant.36.clone.1), dimensions={1}, to_apply=%region_5.6 | reduce | flops 262144 | bytes 2621444 | tf_op jit(solution)/shard_map/reduce_sum | solution.py:358
  373.7 0.2 slice.56
  373.9 0.3 reshape.203
  374.2 3.7 reduce.1
  377.9 3.0 reduce_sum.58
  (11 shorter events, 0.1 us)
Async XLA Ops:
  0.6 5.8 %copy-start.1 = (bf16[128,2048]{1,0:T(8,128)(2,1)S(1)}, bf16[128,2048]{1,0:T(8,128)(2,1)}, u32[]{:S(2)}) copy-start(bf16[128,2048]{1,0:T(8,128)(2,1)} %param.7) | copy-start | bytes 1572868
  6.6 2.2 copy-start.2
  11.8 1.8 copy-start.3
  11.9 1.8 copy-start.4
  163.6 3.5 copy-start
  167.1 2.5 slice-start
  167.5 3.2 slice-start.1
  167.5 3.4 slice-start.2
  181.5 179.3 %copy-start.5 = (s32[128,2]{0,1:T(2,128)S(1)}, s32[128,2]{0,1:T(2,128)}, u32[]{:S(2)}) copy-start(s32[128,2]{0,1:T(2,128)} %param.8) | copy-start | bytes 3076
